TPU v7x, 256 devices: a whole 4x4x8 slice. The times are simulated.
256 devices in a mesh: pairs: 32 (over z, x), sect: 8 (over y, core).
Axes of the slice: x: 4, y: 4, z: 8, core: 2. Of those that a mesh axis runs over, the one named last changes fastest.
Arguments:
- wavefunction: bfloat16 [8192, 1024], P('sect'), may hold values from -6 to 6
- left_normal: bfloat16 [64, 16, 512, 512], P('pairs', 'sect'), may hold values from -0.03125 to 0.03125
- left_comp: bfloat16 [64, 16, 512, 512], P('pairs', 'sect'), may hold values from -0.03125 to 0.03125
- right_comp: bfloat16 [64, 2, 512, 512], P('pairs'), may hold values from -0.25 to 0.25
- right_normal: bfloat16 [64, 2, 512, 512], P('pairs'), may hold values from -0.25 to 0.25
- pair_shift: int32 [64], P('pairs'), may hold values from 0 to 1
- pair_count: int32 [32], P('pairs'), may hold values from 1 to 2, as said below
- sector_rows: int32 [16], P('sect'), may hold values from 128 to 512, as said below
Outputs:
- sigma: bfloat16 [8192, 1024], P(('sect', 'pairs'))
Inputs may be any that keep to these rules, and one draw needn't show every extreme that they name: Index i of pairs holds pair slots i * 2 to (i + 1) * 2 - 1, of which the first pair_count[i] are live; some index has all 2 live. Rows of sector s at or beyond sector_rows[s] are padding; some sector uses all 512 rows.
All inputs are finite; a program needn't handle non-finite values.
Results may differ from a plain program's by a relative error of at most 0.005.
Values may be sent and summed in bfloat16 or wider, within the bound.
No kernel may reach another device: no remote copies, remote signals or barrier semaphores. Data moves between devices by JAX's collectives and lax.ppermute only.
A program may use at most 128 MiB of HBM per device.

v0:
```python
import jax
import jax.numpy as jnp
from jax import lax
from jax.sharding import PartitionSpec as P


def shifted(value, axis, steps):
    count = lax.axis_size(axis)
    leading, last = (max(0, -steps), min(count, count - steps))
    return lax.ppermute(value, axis, [(source, source + steps) for source in range(leading, last)])


def local(
    wavefunction,
    left_normal,
    left_comp,
    right_comp,
    right_normal,
    pair_shift,
    pair_count,
    sector_rows,
):
    sec_dev = left_normal.shape[1]
    width = left_normal.shape[3]
    blocks = right_comp.shape[1]
    block_width = right_comp.shape[3]
    columns = blocks * block_width
    row_keep = jnp.arange(width, dtype=jnp.int32)[None, :] < sector_rows[:, None]
    blocked = wavefunction.reshape(sec_dev, width, columns)
    masked = jnp.where(row_keep[:, :, None], blocked, jnp.zeros((), jnp.bfloat16))
    lower_block = shifted(masked[sec_dev - 1], "sect", 1)
    earlier = jnp.concatenate([lower_block[None], masked[: sec_dev - 1]], axis=0)

    def right_apply(left_part, offset, right_ops):
        rolled = jnp.roll(left_part.reshape(sec_dev, width, blocks, block_width), -offset, axis=2)
        product = jnp.einsum(
            "sikb,kcb->sikc", rolled, right_ops, preferred_element_type=jnp.float32
        )
        return product.reshape(sec_dev * width, columns)

    def add_pair(slot_index, totals):
        normal_left = jnp.einsum(
            "sij,sjk->sik", left_normal[slot_index], masked, preferred_element_type=jnp.float32
        ).astype(jnp.bfloat16)
        comp_left = jnp.einsum(
            "sij,sjk->sik", left_comp[slot_index], earlier, preferred_element_type=jnp.float32
        ).astype(jnp.bfloat16)
        offset = pair_shift[slot_index]
        normal_next = totals[0] + right_apply(normal_left, offset, right_comp[slot_index])
        comp_next = totals[1] + right_apply(comp_left, offset, right_normal[slot_index])
        return (normal_next, comp_next)

    empty = jnp.zeros((sec_dev * width, columns), jnp.float32)
    normal_sum, comp_sum = lax.fori_loop(0, pair_count[0], add_pair, (empty, empty))
    normal_part = lax.psum_scatter(normal_sum, "pairs", scatter_dimension=0, tiled=True)
    comp_part = lax.psum_scatter(comp_sum, "pairs", scatter_dimension=0, tiled=True)
    combined = normal_part + comp_part
    own_rows = combined.shape[0]
    row_start = lax.axis_index("pairs") * own_rows
    keep_flat = row_keep.reshape(sec_dev * width)
    keep_mine = lax.dynamic_slice_in_dim(keep_flat, row_start, own_rows, 0)
    combined = jnp.where(keep_mine[:, None], combined, jnp.zeros((), jnp.float32))
    return combined.astype(jnp.bfloat16)


def solution(mesh):
    placed = (
        P("sect", None),
        P("pairs", "sect", None, None),
        P("pairs", "sect", None, None),
        P("pairs", None, None, None),
        P("pairs", None, None, None),
        P("pairs"),
        P("pairs"),
        P("sect"),
    )
    return jax.shard_map(
        local, mesh=mesh, in_specs=placed, out_specs=P(("sect", "pairs"), None), check_vma=False
    )
```

profile of v0, /device:TPU:56, one launch (start us, length us, event | category | flops | bytes accessed | tf_op | source)
XLA Modules:
  0.0 359.7 jit_solution(16995141858658383858)
XLA Ops:
  10.3 1.9 collective-permute-start
  12.2 14.5 %collective-permute-done = bf16[512,1024]{1,0:T(8,128)(2,1)} collective-permute-done((bf16[512,1024]{1,0:T(8,128)(2,1)}, bf16[512,1024]{1,0:T(8,128)(2,1)}, u32[]{:S(2)}, u32[]{:S(2)}) %collective-permute-start) | collective-permute-done | bytes 1048608 | tf_op jit(solution)/shard_map/ppermute | solution.py:10
  26.7 2.7 pad_maximum_fusion
  29.4 2.5 broadcast_in_dim.35.clone
  31.9 2.5 broadcast_in_dim.35
  34.4 87.4 %while.12 = (s32[]{:T(128)}, f32[1024,1024]{1,0:T(8,128)}, f32[1024,1024]{1,0:T(8,128)}, s32[]{:T(128)}, bf16[2,2,512,512]{3,2,1,0:T(8,128)(2,1)}, /*index=5*/bf...) while((s32[]{:T(128)}, f32[1024,1024]{1,0:T(8,128)}, ...), condition=%wide.region_1.3_spmd, body=%wide.region_0.2_spmd.sunk | while | flops 4307550208 | bytes 184549968 | solution.py:54
  36.3 3.2 convolution_convert_fusion.5
  41.0 3.3 convolution_bitcast_fusion.5
  44.3 7.3 %copy.39 = f32[2,512,2,512]{3,2,1,0:T(2,128)} copy(f32[2,512,2,512]{1,3,0,2:T(8,128)} %convolution_bitcast_fusion.5) | data formatting | bytes 8388608 | tf_op jit(solution)/shard_map/while/body/sikb,kcb->sikc/transpose | solution.py:36
  51.7 3.4 copy.40
  60.3 3.3 convolution_bitcast_fusion.4
  63.6 7.3 %copy.36 = f32[2,512,2,512]{3,2,1,0:T(2,128)} copy(f32[2,512,2,512]{1,3,0,2:T(8,128)} %convolution_bitcast_fusion.4) | data formatting | bytes 8388608 | tf_op jit(solution)/shard_map/while/body/sikb,kcb->sikc/transpose | solution.py:36
  70.9 3.4 copy.37
  75.8 1.9 copy-done.3
  79.6 3.2 convolution_convert_fusion.5
  84.4 3.3 convolution_bitcast_fusion.5
  87.7 7.3 %copy.39 = f32[2,512,2,512]{3,2,1,0:T(2,128)} copy(f32[2,512,2,512]{1,3,0,2:T(8,128)} %convolution_bitcast_fusion.5) | data formatting | bytes 8388608 | tf_op jit(solution)/shard_map/while/body/sikb,kcb->sikc/transpose | solution.py:36
  95.0 3.4 copy.40
  103.6 3.3 convolution_bitcast_fusion.4
  106.9 7.3 %copy.36 = f32[2,512,2,512]{3,2,1,0:T(2,128)} copy(f32[2,512,2,512]{1,3,0,2:T(8,128)} %convolution_bitcast_fusion.4) | data formatting | bytes 8388608 | tf_op jit(solution)/shard_map/while/body/sikb,kcb->sikc/transpose | solution.py:36
  114.2 3.4 copy.37
  119.2 1.9 copy-done.3
  121.8 6.8 %add.38 = f32[1024,1024]{1,0:T(8,128)} add(f32[1024,1024]{1,0:T(8,128)} %get-tuple-element.65, f32[1024,1024]{1,0:T(8,128)} %get-tuple-element.66) | non-fusion elementwise | flops 1048576 | bytes 12582912 | tf_op jit(solution)/shard_map/add | solution.py:57
  128.7 222.5 %reduce-scatter.2.cloned.1.call-done = f32[32,1024]{1,0:T(8,128)} async-done(((f32[1024,1024]{1,0:T(8,128)}), f32[32,1024]{1,0:T(8,128)}) %reduce-scatter.2.cloned.1.call-update) | async-done | bytes 131088 | tf_op jit(solution)/shard_map/reduce_scatter | solution.py:55
  (48 shorter events, 23.3 us)
Async XLA Ops:
  6.5 344.7 %reduce-scatter.2.cloned.1.call-start = ((), (), s32[]{:S(2)}) async-start(), calls=%async_computation.1 | async-start | bytes 4325376 | tf_op jit(solution)/shard_map/reduce_scatter | solution.py:55
  10.3 16.4 %collective-permute-start = (bf16[512,1024]{1,0:T(8,128)(2,1)}, bf16[512,1024]{1,0:T(8,128)(2,1)}, u32[]{:S(2)}, u32[]{:S(2)}) collective-permute-start(bf16[512,1024]{1,0:T(8,128)(2,1)} %get-tuple-element.89), channel_id=1, source_target_pairs={{0,1},{1,2},{2,3},{3,4},{4,5},{5,6},{6,7},{8,9},{9,10},{10,11},{11... | collective-permute-start | bytes 3145736 | tf_op jit(solution)/shard_map/ppermute | solution.py:10
  31.9 2.5 copy-start.7
  39.4 1.6 copy-start.6
  51.7 3.4 copy-start
  55.1 1.6 copy-start.5
  56.7 2.0 copy-start.1
  58.7 1.6 copy-start.4
  70.9 3.4 copy-start.2
  75.8 2.0 copy-start.3
  82.8 1.6 copy-start.6
  95.0 3.4 copy-start
  98.5 1.6 copy-start.5
  100.1 2.0 copy-start.1
  102.0 1.6 copy-start.4
  114.2 3.4 copy-start.2
  119.2 2.0 copy-start.3
Sparse Core Ops, SparseCore 0:
  128.7 222.4 reduce-scatter.1
where the time goes:
time: 362 us; the launch traced here: 360 us
  waiting for transfers between devices  237 us (65%)
  local copies, waits for them, and re-layouts  62.2 us (17%)
  matrix products  22.1 us (6%)
  other arithmetic  19.6 us (5%)
  between operations  13.4 us (4%)
    reduce_scatter x1, waiting for transfers between devices, local(): lax.psum_scatter(normal_sum, 'pairs', scatter_dimension=0, tiled=True)  223 us
    transpose x4, local copies, waits for them, and re-layouts, right_apply(): jnp.einsum('sikb,kcb->sikc', rolled, right_ops, preferred_element_type=jn...  29.2 us
    while x32, local copies, waits for them, and re-layouts  24.9 us
    ppermute x1, waiting for transfers between devices, shifted(): lax.ppermute(value, axis, [(source, source + steps) for source in range(l...  14.5 us
    dot_general x4, matrix products, right_apply(): jnp.einsum('sikb,kcb->sikc', rolled, right_ops, preferred_element_type=jn...  13.2 us
  transfers between devices with their start and end apart: 2, of which 2 were waited for; matrix products, arithmetic and copies ran while one was open for 0% of the time, Pallas kernels for 0%

commit v1 on v0

v1 whole, which is shorter than its diff:
```python
import jax
import jax.numpy as jnp
from jax import lax
from jax.experimental import pallas as pl
from jax.experimental.pallas import tpu as pltpu
from jax.sharding import PartitionSpec as P

B = 512
KB = 512
K = 1024
NP = 2
X_DEV = 4
ROW = 32
BF = jnp.bfloat16
F32 = jnp.float32
ANY = pl.BlockSpec(memory_space=pl.ANY)
SMEM = pl.BlockSpec(memory_space=pltpu.SMEM)
VMEM = pl.BlockSpec(memory_space=pltpu.VMEM)


def sector_call(name, terms, masked, pair_shift, pair_count, sector_rows, init=None, order=None):
    count = len(terms)
    have_init = init is not None

    def body(*refs):
        refs = list(refs)
        shift, live, rows = refs[:3]
        ins = refs[3 : 3 + 3 * count]
        pos = 3 + 3 * count
        init_ref = None
        if have_init:
            init_ref = refs[pos]
            pos += 1
        outs = refs[pos : pos + (2 if order else 1)]
        pos += len(outs)
        raw, msk, lft, rgt, acc, sems = refs[pos:]

        def src_copy(t):
            part = terms[t][1]
            return pltpu.make_async_copy(
                ins[3 * t].at[pl.ds(part * B, B), :], raw.at[t], sems.at[0, t]
            )

        def left_copy(p, t):
            return pltpu.make_async_copy(
                ins[3 * t + 1].at[p, terms[t][3]], lft.at[p, t], sems.at[1 + p, t]
            )

        def right_copy(p, t):
            return pltpu.make_async_copy(ins[3 * t + 2].at[p], rgt.at[p, t], sems.at[3 + p, t])

        def init_copy():
            return pltpu.make_async_copy(init_ref, acc, sems.at[5, 0])

        for t in range(count):
            src_copy(t).start()
            left_copy(0, t).start()
            right_copy(0, t).start()
        if have_init:
            init_copy().start()

        @pl.when(live[0] > 1)
        def _():
            for t in range(count):
                left_copy(1, t).start()
                right_copy(1, t).start()

        def work(p):
            for t in range(count):
                if p == 0:
                    src_copy(t).wait()
                    for h in range(2):
                        value = raw[t, :, h * KB : (h + 1) * KB]
                        if masked[t] is not None:
                            at = lax.broadcasted_iota(jnp.int32, (B, KB), 0)
                            value = jnp.where(at < rows[masked[t]], value, jnp.zeros((), BF))
                        msk[t, h] = value
                left_copy(p, t).wait()
                right_copy(p, t).wait()
                if have_init and p == 0 and t == 0:
                    init_copy().wait()
                for j in range(2):
                    half = (j + shift[p]) % 2
                    inner = jnp.dot(
                        lft[p, t], msk[t, half], preferred_element_type=F32
                    ).astype(BF)
                    outer = lax.dot_general(
                        inner, rgt[p, t, j], (((1,), (1,)), ((), ())), preferred_element_type=F32
                    ).reshape(16, ROW, KB)
                    if p == 0 and t == 0 and not have_init:
                        acc[j] = outer
                    else:
                        acc[j] = acc[j] + outer

        work(0)

        @pl.when(live[0] > 1)
        def _():
            work(1)

        if order is None:
            for j in range(2):
                outs[0][j] = acc[j]
        else:
            index = lax.axis_index("pairs")
            my_x = index % X_DEV
            my_z = (index // X_DEV) % 4
            for j in range(2):
                for place, rel in enumerate(order):
                    for zrel in range(4):
                        block = (my_z ^ zrel) * X_DEV + (my_x ^ rel)
                        value = acc[j, block]
                        cols = slice(j * KB, (j + 1) * KB)
                        if place < 2:
                            outs[0][place, zrel, :, cols] = value
                        else:
                            outs[1][place - 2, zrel, :, cols] = value.astype(BF)

    operands = [pair_shift, pair_count, sector_rows]
    for t in terms:
        operands += [t[0], t[2], t[4]]
    if have_init:
        operands.append(init)
    if order is None:
        out_shape = jax.ShapeDtypeStruct((2, 16, ROW, KB), F32)
        out_specs = VMEM
    else:
        out_shape = (
            jax.ShapeDtypeStruct((2, 4, ROW, K), F32),
            jax.ShapeDtypeStruct((2, 4, ROW, K), BF),
        )
        out_specs = (VMEM, VMEM)
    return pl.pallas_call(
        body,
        name=name,
        out_shape=out_shape,
        in_specs=[SMEM] * 3 + [ANY] * (len(operands) - 3),
        out_specs=out_specs,
        scratch_shapes=[
            pltpu.VMEM((count, B, K), BF),
            pltpu.VMEM((count, 2, B, KB), BF),
            pltpu.VMEM((NP, count, B, B), BF),
            pltpu.VMEM((NP, count, 2, KB, KB), BF),
            pltpu.VMEM((2, 16, ROW, KB), F32),
            pltpu.SemaphoreType.DMA((6, count)),
        ],
        compiler_params=pltpu.CompilerParams(vmem_limit_bytes=40 * 2**20),
        cost_estimate=pl.CostEstimate(
            flops=count * NP * 4 * B * B * K,
            bytes_accessed=count * 4 * 2**20 + 2 * 2**20,
            transcendentals=0,
        ),
    )(*operands)


def swap(value, mask):
    size = lax.axis_size("pairs")
    return lax.ppermute(value, "pairs", [(i, i ^ mask) for i in range(size)])


def local(
    wavefunction,
    left_normal,
    left_comp,
    right_comp,
    right_normal,
    pair_shift,
    pair_count,
    sector_rows,
):
    sects = lax.axis_size("sect")
    row_ids = jnp.arange(B, dtype=jnp.int32)
    last = jnp.where((row_ids < sector_rows[1])[:, None], wavefunction[B:], jnp.zeros((), BF))
    lower = lax.ppermute(last, "sect", [(i, i + 1) for i in range(sects - 1)])
    scal = (pair_shift, pair_count, sector_rows)

    keep_b, send_b = sector_call(
        "upper",
        [
            (wavefunction, 1, left_normal, 1, right_comp),
            (wavefunction, 0, left_comp, 1, right_normal),
        ],
        [1, 0],
        *scal,
        order=(0, 3, 1, 2),
    )
    part_a = sector_call(
        "lower_normal", [(wavefunction, 0, left_normal, 0, right_comp)], [0], *scal
    )
    keep_a, send_a = sector_call(
        "lower_comp",
        [(lower, 0, left_comp, 0, right_normal)],
        [None],
        *scal,
        init=part_a,
        order=(0, 1, 3, 2),
    )

    def x_stage(keep, send, first, second):
        got = swap(send, first)
        next_send = (keep[1] + got[1].astype(F32)).astype(BF)
        got_next = swap(next_send, second)
        return keep[0] + got[0].astype(F32) + got_next.astype(F32)

    sum_b = x_stage(keep_b, send_b, 1, 3)
    sum_a = x_stage(keep_a, send_a, 3, 1)

    index = lax.axis_index("pairs")
    high = (index // (4 * X_DEV)) % 2 == 1
    send = jnp.stack([sum_a[1], sum_a[3], sum_b[1], sum_b[3]]).astype(BF)
    got = swap(send, 1 * X_DEV).astype(F32)
    a0, a2, b0, b2 = sum_a[0] + got[0], sum_a[2] + got[1], sum_b[0] + got[2], sum_b[2] + got[3]
    own0, own2 = jnp.where(high, b0, a0), jnp.where(high, b2, a2)
    oth0, oth2 = jnp.where(high, a0, b0), jnp.where(high, a2, b2)
    got = swap(jnp.stack([own2, oth0]).astype(BF), 2 * X_DEV).astype(F32)
    own = own0 + got[0]
    got = swap((oth2 + got[1]).astype(BF), 6 * X_DEV).astype(F32)
    own = own + got
    used = jnp.where(high, sector_rows[1], sector_rows[0])
    row = (index % 16) * ROW + jnp.arange(ROW, dtype=jnp.int32)
    return jnp.where((row < used)[:, None], own, jnp.zeros((), F32)).astype(BF)


def solution(mesh):
    placed = (
        P("sect", None),
        P("pairs", "sect", None, None),
        P("pairs", "sect", None, None),
        P("pairs", None, None, None),
        P("pairs", None, None, None),
        P("pairs"),
        P("pairs"),
        P("sect"),
    )
    return jax.shard_map(
        local, mesh=mesh, in_specs=placed, out_specs=P(("sect", "pairs"), None), check_vma=False
    )
```

time: 362 us -> 79 us (0.22)
  the two profiles are of different devices: /device:TPU:56 before, /device:TPU:65 now
where the time goes in v1:
time: 79 us; the launch traced here: 78.5 us
  starting transfers between devices  28.7 us (36%)
  waiting for transfers between devices  28 us (35%)
  Pallas kernels  8.58 us (11%)
  local copies, waits for them, and re-layouts  7.87 us (10%)
  other arithmetic  3.24 us (4%)
  between operations  2.15 us (3%)
    ppermute x7, waiting for transfers between devices, swap(): return lax.ppermute(value, 'pairs', [(i, i ^ mask) for i in range(size)])  28 us
    ppermute x7, starting transfers between devices, swap(): return lax.ppermute(value, 'pairs', [(i, i ^ mask) for i in range(size)])  24.9 us
    pallas_call x3, Pallas kernels, sector_call(): pl.pallas_call(body, name=name, out_shape=out_shape, in_specs=[SMEM] * 3...  8.58 us
    unnamed x18, local copies, waits for them, and re-layouts  6.38 us
    ppermute x1, starting transfers between devices, local(): lower = lax.ppermute(last, 'sect', [(i, i + 1) for i in range(sects - 1)])  3.77 us
  transfers between devices with their start and end apart: 8, of which 6 were waited for; matrix products, arithmetic and copies ran while one was open for 0% of the time, Pallas kernels for 11%

profile of v1, /device:TPU:65, one launch (start us, length us, event | category | flops | bytes accessed | tf_op | source)
XLA Modules:
  0.0 78.5 jit_solution(9707473664011031838)
XLA Ops:
  0.0 1.5 %fusion.12 = (s32[1]{0:T(128)}, s32[1]{0:T(128)}) fusion(s32[2]{0:T(128)} %refs_2_.5), kind=kLoop, calls=%fused_computation.29 | loop fusion | bytes 16 | tf_op jit(solution)/shard_map/slice | solution.py:219
  1.5 0.6 iota_compare_fusion
  2.1 1.4 %slice_select_fusion = bf16[512,1024]{1,0:T(8,128)(2,1)S(1)} fusion(bf16[1024,1024]{1,0:T(8,128)(2,1)} %refs_3_.3, pred[512]{0:T(512)(128)(4,1)S(1)} %iota_compare_fusion), kind=kLoop, calls=%fused_computation | loop fusion | flops 524288 | bytes 2097664 | tf_op jit(solution)/shard_map/jit(_where)/select_n | solution.py:173
  3.5 3.8 %collective-permute-start.2 = (bf16[512,1024]{1,0:T(8,128)(2,1)S(1)}, bf16[512,1024]{1,0:T(8,128)(2,1)S(1)}, u32[]{:S(2)}, u32[]{:S(2)}) collective-permute-start(bf16[512,1024]{1,0:T(8,128)(2,1)S(1)} %slice_select_fusion), channel_id=1, source_target_pairs={{0,1},{1,2},{2,3},{3,4},{4,5},{5,6},{6,7},{8,9},{9,10},{10,11},{11... | collective-permute-start | bytes 3145736 | tf_op jit(solution)/shard_map/ppermute | solution.py:174
  7.9 1.6 %copy-done.1 = bf16[2,2,512,512]{3,2,1,0:T(8,128)(2,1)S(1)} copy-done((bf16[2,2,512,512]{3,2,1,0:T(8,128)(2,1)S(1)}, bf16[2,2,512,512]{3,2,1,0:T(8,128)(2,1)}, u32[]{:S(2)}) %copy-start.1) | copy-done | bytes 2097176
  9.5 1.6 %copy-done.2 = bf16[2,2,512,512]{3,2,1,0:T(8,128)(2,1)S(1)} copy-done((bf16[2,2,512,512]{3,2,1,0:T(8,128)(2,1)S(1)}, bf16[2,2,512,512]{3,2,1,0:T(8,128)(2,1)}, u32[]{:S(2)}) %copy-start.2) | copy-done | bytes 2097176
  11.1 1.6 %copy-done.5 = bf16[2,2,512,512]{3,2,1,0:T(8,128)(2,1)S(1)} copy-done((bf16[2,2,512,512]{3,2,1,0:T(8,128)(2,1)S(1)}, bf16[2,2,512,512]{3,2,1,0:T(8,128)(2,1)}, u32[]{:S(2)}) %copy-start.5) | copy-done | bytes 2097176
  12.7 1.6 %copy-done.7 = bf16[2,2,512,512]{3,2,1,0:T(8,128)(2,1)S(1)} copy-done((bf16[2,2,512,512]{3,2,1,0:T(8,128)(2,1)S(1)}, bf16[2,2,512,512]{3,2,1,0:T(8,128)(2,1)}, u32[]{:S(2)}) %copy-start.7) | copy-done | bytes 2097176
  14.3 3.9 %upper.1 = (f32[2,4,32,1024]{3,2,1,0:T(8,128)S(1)}, bf16[2,4,32,1024]{3,2,1,0:T(8,128)(2,1)S(1)}) custom-call(s32[2]{0:T(128)S(1)} %copy-done.4, s32[1]{0:T(128)S(6)} %copy.9.refs_1_, s32[2]{0:T(128)S(1)} %copy-done.3, bf16[1024,1024]{1,0:T(8,128)(2,1)S(1)} %copy-done, bf16[2,2,512,512]{3,2,1,0:T(8,128)(2,1)S(1)} %copy-done.1, ...), custom_call_target="tpu_custom_call" | custom-call | flops 4294967296 | bytes 10485760 | tf_op jit(solution)/shard_map/upper/pallas_call | solution.py:133
  18.2 1.3 %collective-permute-start = (bf16[2,4,32,1024]{3,2,1,0:T(8,128)(2,1)S(1)}, bf16[2,4,32,1024]{3,2,1,0:T(8,128)(2,1)S(1)}, u32[]{:S(2)}, u32[]{:S(2)}) collective-permute-start(bf16[2,4,32,1024]{3,2,1,0:T(8,128)(2,1)S(1)} %get-tuple-element.10), channel_id=1, source_target_pairs={{0,8},{8,0},{16,24},{24,16},{32,40},{40,32},{48,56},{56,48},{64,72... | collective-permute-start | bytes 1572872 | tf_op jit(solution)/shard_map/ppermute | solution.py:158
  19.5 2.3 %lower_normal.1.refs_6_ = f32[2,16,32,512]{3,2,1,0:T(8,128)S(1)} custom-call(s32[2]{0:T(128)S(1)} %copy-done.4, s32[1]{0:T(128)S(6)} %copy.9.refs_1_, s32[2]{0:T(128)S(1)} %copy-done.3, bf16[1024,1024]{1,0:T(8,128)(2,1)S(1)} %copy-done, bf16[2,2,512,512]{3,2,1,0:T(8,128)(2,1)S(1)} %copy-done.1, bf16[2,2,512,512]{3,2,1,0:T(8,128)(2,1)S(1)} %copy-done.2), custom_call_target="tpu_custom_call" | custom-call | flops 2147483648 | bytes 6291456 | tf_op jit(solution)/shard_map/lower_normal/pallas_call | solution.py:133
  21.8 2.4 %lower_comp.1 = (f32[2,4,32,1024]{3,2,1,0:T(8,128)S(1)}, bf16[2,4,32,1024]{3,2,1,0:T(8,128)(2,1)S(1)}) custom-call(s32[2]{0:T(128)S(1)} %copy-done.4, s32[1]{0:T(128)S(6)} %copy.9.refs_1_, s32[2]{0:T(128)S(1)} %copy-done.3, bf16[512,1024]{1,0:T(8,128)(2,1)S(1)} %collective-permute-done.2.refs_3_, bf16[2,2,512,512]{3,2,1,0:T(8,128)(2,1)S(1)} %copy-done.6, ...), custom_call_target="tpu_custom_call" | custom-call | flops 2147483648 | bytes 6291456 | tf_op jit(solution)/shard_map/lower_comp/pallas_call | solution.py:133
  24.3 7.4 %collective-permute-start.3 = (bf16[2,4,32,1024]{3,2,1,0:T(8,128)(2,1)S(1)}, bf16[2,4,32,1024]{3,2,1,0:T(8,128)(2,1)S(1)}, u32[]{:S(2)}, u32[]{:S(2)}) collective-permute-start(bf16[2,4,32,1024]{3,2,1,0:T(8,128)(2,1)S(1)} %get-tuple-element.12), channel_id=1, source_target_pairs={{0,24},{8,16},{16,8},{24,0},{32,56},{40,48},{48,40},{56,32},{64,88... | collective-permute-start | bytes 1572872 | tf_op jit(solution)/shard_map/ppermute | solution.py:158
  31.7 5.1 %collective-permute-start.1 = (bf16[4,32,1024]{2,1,0:T(8,128)(2,1)S(1)}, bf16[4,32,1024]{2,1,0:T(8,128)(2,1)S(1)}, u32[]{:S(2)}, u32[]{:S(2)}) collective-permute-start(bf16[4,32,1024]{2,1,0:T(8,128)(2,1)S(1)} %fusion), channel_id=1, source_target_pairs={{0,24},{8,16},{16,8},{24,0},{32,56},{40,48},{48,40},{56,32},{64,88... | collective-permute-start | bytes 786440 | tf_op jit(solution)/shard_map/ppermute | solution.py:158
  36.8 7.3 %collective-permute-done.3 = bf16[2,4,32,1024]{3,2,1,0:T(8,128)(2,1)S(1)} collective-permute-done((bf16[2,4,32,1024]{3,2,1,0:T(8,128)(2,1)S(1)}, bf16[2,4,32,1024]{3,2,1,0:T(8,128)(2,1)S(1)}, u32[]{:S(2)}, u32[]{:S(2)}) %collective-permute-start.3) | collective-permute-done | bytes 524320 | tf_op jit(solution)/shard_map/ppermute | solution.py:158
  44.1 0.4 collective-permute-start.4
  44.5 4.1 %collective-permute-done.1 = bf16[4,32,1024]{2,1,0:T(8,128)(2,1)S(1)} collective-permute-done((bf16[4,32,1024]{2,1,0:T(8,128)(2,1)S(1)}, bf16[4,32,1024]{2,1,0:T(8,128)(2,1)S(1)}, u32[]{:S(2)}, u32[]{:S(2)}) %collective-permute-start.1) | collective-permute-done | bytes 262176 | tf_op jit(solution)/shard_map/ppermute | solution.py:158
  48.7 2.8 %collective-permute-done.4 = bf16[4,32,1024]{2,1,0:T(8,128)(2,1)S(1)} collective-permute-done((bf16[4,32,1024]{2,1,0:T(8,128)(2,1)S(1)}, bf16[4,32,1024]{2,1,0:T(8,128)(2,1)S(1)}, u32[]{:S(2)}, u32[]{:S(2)}) %collective-permute-start.4) | collective-permute-done | bytes 262176 | tf_op jit(solution)/shard_map/ppermute | solution.py:158
  51.7 1.7 %collective-permute-start.5 = (bf16[4,32,1024]{2,1,0:T(8,128)(2,1)S(1)}, bf16[4,32,1024]{2,1,0:T(8,128)(2,1)S(1)}, u32[]{:S(2)}, u32[]{:S(2)}) collective-permute-start(bf16[4,32,1024]{2,1,0:T(8,128)(2,1)S(1)} %pad_maximum_fusion), channel_id=1, source_target_pairs={{0,32},{8,40},{16,48},{24,56},{32,0},{40,8},{48,16},{56,24},{64,96... | collective-permute-start | bytes 786440 | tf_op jit(solution)/shard_map/ppermute | solution.py:158
  53.4 6.6 %collective-permute-done.5 = bf16[4,32,1024]{2,1,0:T(8,128)(2,1)S(1)} collective-permute-done((bf16[4,32,1024]{2,1,0:T(8,128)(2,1)S(1)}, bf16[4,32,1024]{2,1,0:T(8,128)(2,1)S(1)}, u32[]{:S(2)}, u32[]{:S(2)}) %collective-permute-start.5) | collective-permute-done | bytes 262176 | tf_op jit(solution)/shard_map/ppermute | solution.py:158
  61.5 4.0 %collective-permute-done.6 = bf16[2,32,1024]{2,1,0:T(8,128)(2,1)S(1)} collective-permute-done((bf16[2,32,1024]{2,1,0:T(8,128)(2,1)S(1)}, bf16[2,32,1024]{2,1,0:T(8,128)(2,1)S(1)}, u32[]{:S(2)}, u32[]{:S(2)}) %collective-permute-start.6) | collective-permute-done | bytes 131104 | tf_op jit(solution)/shard_map/ppermute | solution.py:158
  65.6 9.0 %collective-permute-start.7 = (bf16[32,1024]{1,0:T(8,128)(2,1)S(1)}, bf16[32,1024]{1,0:T(8,128)(2,1)S(1)}, u32[]{:S(2)}, u32[]{:S(2)}) collective-permute-start(bf16[32,1024]{1,0:T(8,128)(2,1)S(1)} %fusion.7), channel_id=1, source_target_pairs={{0,192},{8,200},{16,208},{24,216},{32,224},{40,232},{48,240},{56,2... | collective-permute-start | bytes 196616 | tf_op jit(solution)/shard_map/ppermute | solution.py:158
  74.6 3.2 %collective-permute-done.7 = bf16[32,1024]{1,0:T(8,128)(2,1)S(1)} collective-permute-done((bf16[32,1024]{1,0:T(8,128)(2,1)S(1)}, bf16[32,1024]{1,0:T(8,128)(2,1)S(1)}, u32[]{:S(2)}, u32[]{:S(2)}) %collective-permute-start.7) | collective-permute-done | bytes 65568 | tf_op jit(solution)/shard_map/ppermute | solution.py:158
  77.8 0.7 fusion.6
  (29 shorter events, 0.7 us)
Async XLA Ops:
  0.0 7.9 %copy-start.3 = (s32[2]{0:T(128)S(1)}, s32[2]{0:T(128)}, u32[]{:S(2)}) copy-start(s32[2]{0:T(128)} %refs_2_.5) | copy-start | bytes 28
  0.0 7.9 %copy-start = (bf16[1024,1024]{1,0:T(8,128)(2,1)S(1)}, bf16[1024,1024]{1,0:T(8,128)(2,1)}, u32[]{:S(2)}) copy-start(bf16[1024,1024]{1,0:T(8,128)(2,1)} %refs_3_.3) | copy-start | bytes 6291460
  0.0 7.9 %copy-start.4 = (s32[2]{0:T(128)S(1)}, s32[2]{0:T(128)}, u32[]{:S(2)}) copy-start(s32[2]{0:T(128)} %refs_0_.5) | copy-start | bytes 28
  3.5 18.3 %collective-permute-start.2 = (bf16[512,1024]{1,0:T(8,128)(2,1)S(1)}, bf16[512,1024]{1,0:T(8,128)(2,1)S(1)}, u32[]{:S(2)}, u32[]{:S(2)}) collective-permute-start(bf16[512,1024]{1,0:T(8,128)(2,1)S(1)} %slice_select_fusion), channel_id=1, source_target_pairs={{0,1},{1,2},{2,3},{3,4},{4,5},{5,6},{6,7},{8,9},{9,10},{10,11},{11... | collective-permute-start | bytes 3145736 | tf_op jit(solution)/shard_map/ppermute | solution.py:174
  7.9 1.6 %copy-start.1 = (bf16[2,2,512,512]{3,2,1,0:T(8,128)(2,1)S(1)}, bf16[2,2,512,512]{3,2,1,0:T(8,128)(2,1)}, u32[]{:S(2)}) copy-start(bf16[2,2,512,512]{3,2,1,0:T(8,128)(2,1)} %refs_4_.4) | copy-start | bytes 6291460
  9.5 1.6 %copy-start.2 = (bf16[2,2,512,512]{3,2,1,0:T(8,128)(2,1)S(1)}, bf16[2,2,512,512]{3,2,1,0:T(8,128)(2,1)}, u32[]{:S(2)}) copy-start(bf16[2,2,512,512]{3,2,1,0:T(8,128)(2,1)} %refs_5_.4) | copy-start | bytes 6291460
  11.1 1.6 %copy-start.5 = (bf16[2,2,512,512]{3,2,1,0:T(8,128)(2,1)S(1)}, bf16[2,2,512,512]{3,2,1,0:T(8,128)(2,1)}, u32[]{:S(2)}) copy-start(bf16[2,2,512,512]{3,2,1,0:T(8,128)(2,1)} %refs_4_.5) | copy-start | bytes 6291460
  12.7 1.6 %copy-start.7 = (bf16[2,2,512,512]{3,2,1,0:T(8,128)(2,1)S(1)}, bf16[2,2,512,512]{3,2,1,0:T(8,128)(2,1)}, u32[]{:S(2)}) copy-start(bf16[2,2,512,512]{3,2,1,0:T(8,128)(2,1)} %refs_5_.5) | copy-start | bytes 6291460
  18.2 3.6 %copy-start.6 = (bf16[2,2,512,512]{3,2,1,0:T(8,128)(2,1)S(1)}, bf16[2,2,512,512]{3,2,1,0:T(8,128)(2,1)}, u32[]{:S(2)}) copy-start(bf16[2,2,512,512]{3,2,1,0:T(8,128)(2,1)} %refs_4_.5) | copy-start | bytes 6291460
  18.2 3.6 %copy-start.8 = (bf16[2,2,512,512]{3,2,1,0:T(8,128)(2,1)S(1)}, bf16[2,2,512,512]{3,2,1,0:T(8,128)(2,1)}, u32[]{:S(2)}) copy-start(bf16[2,2,512,512]{3,2,1,0:T(8,128)(2,1)} %refs_5_.5) | copy-start | bytes 6291460
  18.2 13.4 %collective-permute-start = (bf16[2,4,32,1024]{3,2,1,0:T(8,128)(2,1)S(1)}, bf16[2,4,32,1024]{3,2,1,0:T(8,128)(2,1)S(1)}, u32[]{:S(2)}, u32[]{:S(2)}) collective-permute-start(bf16[2,4,32,1024]{3,2,1,0:T(8,128)(2,1)S(1)} %get-tuple-element.10), channel_id=1, source_target_pairs={{0,8},{8,0},{16,24},{24,16},{32,40},{40,32},{48,56},{56,48},{64,72... | collective-permute-start | bytes 1572872 | tf_op jit(solution)/shard_map/ppermute | solution.py:158
  24.3 19.8 %collective-permute-start.3 = (bf16[2,4,32,1024]{3,2,1,0:T(8,128)(2,1)S(1)}, bf16[2,4,32,1024]{3,2,1,0:T(8,128)(2,1)S(1)}, u32[]{:S(2)}, u32[]{:S(2)}) collective-permute-start(bf16[2,4,32,1024]{3,2,1,0:T(8,128)(2,1)S(1)} %get-tuple-element.12), channel_id=1, source_target_pairs={{0,24},{8,16},{16,8},{24,0},{32,56},{40,48},{48,40},{56,32},{64,88... | collective-permute-start | bytes 1572872 | tf_op jit(solution)/shard_map/ppermute | solution.py:158
  31.7 16.9 %collective-permute-start.1 = (bf16[4,32,1024]{2,1,0:T(8,128)(2,1)S(1)}, bf16[4,32,1024]{2,1,0:T(8,128)(2,1)S(1)}, u32[]{:S(2)}, u32[]{:S(2)}) collective-permute-start(bf16[4,32,1024]{2,1,0:T(8,128)(2,1)S(1)} %fusion), channel_id=1, source_target_pairs={{0,24},{8,16},{16,8},{24,0},{32,56},{40,48},{48,40},{56,32},{64,88... | collective-permute-start | bytes 786440 | tf_op jit(solution)/shard_map/ppermute | solution.py:158
  44.1 7.4 %collective-permute-start.4 = (bf16[4,32,1024]{2,1,0:T(8,128)(2,1)S(1)}, bf16[4,32,1024]{2,1,0:T(8,128)(2,1)S(1)}, u32[]{:S(2)}, u32[]{:S(2)}) collective-permute-start(bf16[4,32,1024]{2,1,0:T(8,128)(2,1)S(1)} %fusion.1), channel_id=1, source_target_pairs={{0,8},{8,0},{16,24},{24,16},{32,40},{40,32},{48,56},{56,48},{64,72... | collective-permute-start | bytes 786440 | tf_op jit(solution)/shard_map/ppermute | solution.py:158
  51.7 8.3 %collective-permute-start.5 = (bf16[4,32,1024]{2,1,0:T(8,128)(2,1)S(1)}, bf16[4,32,1024]{2,1,0:T(8,128)(2,1)S(1)}, u32[]{:S(2)}, u32[]{:S(2)}) collective-permute-start(bf16[4,32,1024]{2,1,0:T(8,128)(2,1)S(1)} %pad_maximum_fusion), channel_id=1, source_target_pairs={{0,32},{8,40},{16,48},{24,56},{32,0},{40,8},{48,16},{56,24},{64,96... | collective-permute-start | bytes 786440 | tf_op jit(solution)/shard_map/ppermute | solution.py:158
  60.2 5.4 %collective-permute-start.6 = (bf16[2,32,1024]{2,1,0:T(8,128)(2,1)S(1)}, bf16[2,32,1024]{2,1,0:T(8,128)(2,1)S(1)}, u32[]{:S(2)}, u32[]{:S(2)}) collective-permute-start(bf16[2,32,1024]{2,1,0:T(8,128)(2,1)S(1)} %pad_maximum_fusion.1), channel_id=1, source_target_pairs={{0,64},{8,72},{16,80},{24,88},{32,96},{40,104},{48,112},{56,120},{... | collective-permute-start | bytes 393224 | tf_op jit(solution)/shard_map/ppermute | solution.py:158
  65.6 12.2 %collective-permute-start.7 = (bf16[32,1024]{1,0:T(8,128)(2,1)S(1)}, bf16[32,1024]{1,0:T(8,128)(2,1)S(1)}, u32[]{:S(2)}, u32[]{:S(2)}) collective-permute-start(bf16[32,1024]{1,0:T(8,128)(2,1)S(1)} %fusion.7), channel_id=1, source_target_pairs={{0,192},{8,200},{16,208},{24,216},{32,224},{40,232},{48,240},{56,2... | collective-permute-start | bytes 196616 | tf_op jit(solution)/shard_map/ppermute | solution.py:158

commit v2 on v0

v2 whole, which is shorter than its diff:
```python
import jax
import jax.numpy as jnp
from jax import lax
from jax.experimental import pallas as pl
from jax.experimental.pallas import tpu as pltpu
from jax.sharding import PartitionSpec as P

B = 512
KB = 512
K = 1024
NP = 2
ROW = 32
SHIFT, ROWS, LIVE = 0, 2, 4
BF = jnp.bfloat16
F32 = jnp.float32
ANY = pl.BlockSpec(memory_space=pl.ANY)
HBM = pl.BlockSpec(memory_space=pltpu.HBM)
SMEM = pl.BlockSpec(memory_space=pltpu.SMEM)
VMEM = pl.BlockSpec(memory_space=pltpu.VMEM)


NT = (((1,), (1,)), ((), ()))


def masked_rows(value, first_row, used):
    at = lax.broadcasted_iota(jnp.int32, value.shape, 0) + first_row
    return jnp.where(at < used, value, jnp.zeros((), BF))


def for_live(live, act):
    for pairs in range(1, NP + 1):

        @pl.when(live == pairs)
        def _():
            act(pairs)


def left_product(left, source, inner, shift, pairs, terms, term):
    out = jnp.dot(left, source[...], preferred_element_type=F32).astype(BF)
    rows = out.shape[0] // pairs
    for p in range(pairs):
        for half in range(2):
            at = (p * terms + term) * KB
            inner[(half + shift[p]) & 1, :, at : at + KB] = out[
                p * rows : (p + 1) * rows, half * KB : (half + 1) * KB
            ]


def row_groups(places):
    index = lax.axis_index("pairs")
    my_x, parity = index & 3, (index >> 2) & 1
    first, second = pair_order(lax.axis_index("sect"))
    rels = (0, second, first, 2)
    return [
        (2 * (zplace % 2) + (parity ^ (zplace // 2))) * 4 + (my_x ^ rels[place])
        for place in places
        for zplace in range(4)
    ]


def cost(flops, mib):
    return pl.CostEstimate(flops=flops, bytes_accessed=mib * 2**20, transcendentals=0)


def limit(mib):
    return pltpu.CompilerParams(vmem_limit_bytes=mib * 2**20)


def mask_last(sector_rows, wavefunction):
    chunk = B // 4

    def body(rows_ref, wave, out, buf, rows, sems):
        copies = [
            pltpu.make_async_copy(
                wave.at[pl.ds(B + c * chunk, chunk), :], buf.at[pl.ds(c * chunk, chunk), :], sems.at[c]
            )
            for c in range(4)
        ]
        count = pltpu.make_async_copy(rows_ref, rows, sems.at[4])
        count.start()
        for copy in copies:
            copy.start()
        count.wait()
        for c, copy in enumerate(copies):
            copy.wait()
            part = slice(c * chunk, (c + 1) * chunk)
            out[part, :] = masked_rows(buf[part, :], c * chunk, rows[1])

    return pl.pallas_call(
        body,
        name="mask_last",
        out_shape=jax.ShapeDtypeStruct((B, K), BF),
        in_specs=[HBM] * 2,
        out_specs=VMEM,
        scratch_shapes=[
            pltpu.VMEM((B, K), BF),
            pltpu.SMEM((2,), jnp.int32),
            pltpu.SemaphoreType.DMA((5,)),
        ],
        compiler_params=limit(8),
        cost_estimate=cost(B * K, 2),
    )(sector_rows, wavefunction)


def upper_call(pair_count, pair_shift, sector_rows, mask_b, wavefunction, left_normal, left_comp, right_comp, right_normal):
    def body(
        cnt, shift_ref, rows_ref, m_b, wave, ln, lc, rc, rn,
        keep, send, scal, m_a, l_na, l_ca, right,
        raw, l_nb, l_cb, inner, acc, shift, rows, sems,
    ):
        wave_copy = pltpu.make_async_copy(wave.at[pl.ds(0, B), :], raw, sems.at[0])

        def left_copies(source, sector, target, size, sem):
            return [
                pltpu.make_async_copy(
                    source.at[p, sector], target.at[pl.ds(p * size, size)], sems.at[sem + p]
                )
                for p in range(NP)
            ]

        def right_copies(source, term, sem):
            return [
                pltpu.make_async_copy(
                    source.at[p], right.at[:, :, pl.ds((p * 2 + term) * KB, KB)], sems.at[sem + p]
                )
                for p in range(NP)
            ]

        normal_b = left_copies(ln, 1, l_nb, B, 1)
        comp_b = left_copies(lc, 1, l_cb, 16, 3)
        rights = right_copies(rc, 0, 5) + right_copies(rn, 1, 7)
        lower = left_copies(ln, 0, l_na, B, 9) + left_copies(lc, 0, l_ca, 16, 11)
        scalars = [
            pltpu.make_async_copy(shift_ref, shift, sems.at[13]),
            pltpu.make_async_copy(rows_ref, rows, sems.at[14]),
        ]
        for copy in scalars + normal_b + [wave_copy] + comp_b + rights:
            copy.start()
        for copy in scalars:
            copy.wait()
        for i in range(2):
            scal[SHIFT + i] = shift[i]
            scal[ROWS + i] = rows[i]
        scal[LIVE] = cnt[0]
        for copy in normal_b:
            copy.wait()
        for_live(
            cnt[0], lambda pairs: left_product(l_nb[: pairs * B, :], m_b, inner, shift, pairs, 2, 0)
        )
        for copy in lower:
            copy.start()
        wave_copy.wait()
        m_a[...] = masked_rows(raw[...], 0, rows[0])
        for copy in comp_b:
            copy.wait()
        for_live(
            cnt[0],
            lambda pairs: left_product(
                l_cb[: pairs * 16].reshape(pairs * B, B), m_a, inner, shift, pairs, 2, 1
            ),
        )
        for copy in rights:
            copy.wait()

        def finish(pairs):
            for j in range(2):
                acc[j] = lax.dot_general(
                    inner[j, :, : 2 * pairs * KB],
                    right[j, :, : 2 * pairs * KB],
                    NT,
                    preferred_element_type=F32,
                ).reshape(16, ROW, KB)

        for_live(cnt[0], finish)
        for i, group in enumerate(row_groups(range(4))):
            for j in range(2):
                cols = slice(j * KB, (j + 1) * KB)
                value = acc[j, group]
                if i < 8:
                    keep[i // 4, i % 4, :, cols] = value
                else:
                    send[i // 4 - 2, i % 4, :, cols] = value.astype(BF)
        for copy in lower:
            copy.wait()

    return pl.pallas_call(
        body,
        name="upper",
        out_shape=(
            jax.ShapeDtypeStruct((2, 4, ROW, K), F32),
            jax.ShapeDtypeStruct((2, 4, ROW, K), BF),
            jax.ShapeDtypeStruct((8,), jnp.int32),
            jax.ShapeDtypeStruct((B, K), BF),
            jax.ShapeDtypeStruct((NP * B, B), BF),
            jax.ShapeDtypeStruct((NP * 16, ROW, B), BF),
            jax.ShapeDtypeStruct((2, KB, 2 * NP * KB), BF),
        ),
        in_specs=[SMEM, HBM, HBM, VMEM] + [HBM] * 5,
        out_specs=(VMEM, VMEM, SMEM) + (VMEM,) * 4,
        scratch_shapes=[
            pltpu.VMEM((B, K), BF),
            pltpu.VMEM((NP * B, B), BF),
            pltpu.VMEM((NP * 16, ROW, B), BF),
            pltpu.VMEM((2, B, 2 * NP * KB), BF),
            pltpu.VMEM((2, 16, ROW, KB), F32),
            pltpu.SMEM((2,), jnp.int32),
            pltpu.SMEM((2,), jnp.int32),
            pltpu.SemaphoreType.DMA((15,)),
        ],
        compiler_params=limit(28),
        cost_estimate=cost(2 * NP * 4 * B * B * K, 10),
    )(
        pair_count,
        pair_shift,
        sector_rows,
        mask_b,
        wavefunction,
        left_normal,
        left_comp,
        right_comp,
        right_normal,
    )


def right_product(inner, right, j, term, pairs):
    ops = [right[j, :, (p * 2 + term) * KB : (p * 2 + term + 1) * KB] for p in range(pairs)]
    return lax.dot_general(
        inner[j, :, : pairs * KB],
        jnp.concatenate(ops, axis=1) if pairs > 1 else ops[0],
        NT,
        preferred_element_type=F32,
    )


def lower_normal(scalars, source, left, right):
    def body(scal, src, lft, rgt, out, inner):
        def act(pairs):
            left_product(lft[: pairs * B, :], src, inner, scal, pairs, 1, 0)
            for j in range(2):
                out[j] = right_product(inner, rgt, j, 0, pairs).reshape(16, ROW, KB)

        for_live(scal[LIVE], act)

    return pl.pallas_call(
        body,
        name="lower_normal",
        out_shape=jax.ShapeDtypeStruct((2, 16, ROW, KB), F32),
        in_specs=[SMEM] + [VMEM] * 3,
        out_specs=VMEM,
        scratch_shapes=[pltpu.VMEM((2, B, NP * KB), BF)],
        compiler_params=limit(20),
        cost_estimate=cost(NP * 4 * B * B * K, 4),
    )(scalars, source, left, right)


def lower_comp(name, places, dtype, scalars, source, left, right, partial):
    def body(scal, src, lft, rgt, part, out, inner):
        groups = row_groups(places)

        def act(pairs):
            rows = [lft[p * 16 + group] for p in range(pairs) for group in groups]
            left_product(jnp.concatenate(rows, axis=0), src, inner, scal, pairs, 1, 0)
            for j in range(2):
                cols = slice(j * KB, (j + 1) * KB)
                total = right_product(inner, rgt, j, 1, pairs).reshape(8, ROW, KB)
                for i, group in enumerate(groups):
                    out[i // 4, i % 4, :, cols] = (part[j, group] + total[i]).astype(dtype)

        for_live(scal[LIVE], act)

    return pl.pallas_call(
        body,
        name=name,
        out_shape=jax.ShapeDtypeStruct((2, 4, ROW, K), dtype),
        in_specs=[SMEM] + [VMEM] * 4,
        out_specs=VMEM,
        scratch_shapes=[pltpu.VMEM((2, B // 2, NP * KB), BF)],
        compiler_params=limit(20),
        cost_estimate=cost(NP * 2 * B * B * K, 4),
    )(scalars, source, left, right, partial)


def pair_order(sect):
    core = sect & 1
    return 1 + 2 * core, 3 - 2 * core


def x_partner(step):
    return lambda x, z, sect: (x ^ pair_order(sect)[step], z)


def z_neighbour(x, z, sect):
    return (x, z ^ 1) if sect & 1 == 0 else (x, (z + 1 if z & 1 else z - 1) % 8)


def z_partner(step):
    return lambda x, z, sect: (x, z ^ (2 * pair_order(sect)[step]))


def swap(value, partner):
    sects = lax.axis_size("sect")
    moves = []
    for index in range(lax.axis_size("pairs")):
        for sect in range(sects):
            x, z = partner(index & 3, index >> 2, sect)
            moves.append((index * sects + sect, (z * 4 + x) * sects + sect))
    return lax.ppermute(value, ("pairs", "sect"), moves)


def local(
    wavefunction,
    left_normal,
    left_comp,
    right_comp,
    right_normal,
    pair_shift,
    pair_count,
    sector_rows,
):
    sects = lax.axis_size("sect")
    (
        wavefunction,
        left_normal,
        left_comp,
        right_comp,
        right_normal,
        pair_shift,
        sector_rows,
    ) = (
        pltpu.with_memory_space_constraint(value, pltpu.HBM)
        for value in (
            wavefunction,
            left_normal,
            left_comp.reshape(NP, 2, 16, ROW, B),
            right_comp,
            right_normal,
            pair_shift,
            sector_rows,
        )
    )
    last = mask_last(sector_rows, wavefunction)
    lower = lax.ppermute(last, "sect", [(i, i + 1) for i in range(sects - 1)])
    keep_b, send_b, scalars, mask_a, left_na, left_ca, right = upper_call(
        pair_count,
        pair_shift,
        sector_rows,
        last,
        wavefunction,
        left_normal,
        left_comp,
        right_comp,
        right_normal,
    )
    part_a = lower_normal(scalars, mask_a, left_na, right)
    comp = (scalars, lower, left_ca, right, part_a)
    send_a = lower_comp("lower_send", (2, 3), BF, *comp)
    keep_a = lower_comp("lower_keep", (0, 1), F32, *comp)

    got_b = swap(send_b, x_partner(0))
    got_a = swap(send_a, x_partner(0))
    got_a, got_b = lax.optimization_barrier((got_a, got_b))
    sum_a = keep_a + got_a.astype(F32)
    send_a = sum_a[1].astype(BF)
    sum_b = keep_b + got_b.astype(F32)
    got_a = swap(send_a, x_partner(1))
    got_b = swap(sum_b[:, 2:].astype(BF), z_neighbour)
    got_a, got_b = lax.optimization_barrier((got_a, got_b))
    sum_a = sum_a[0] + got_a.astype(F32)
    send_a = sum_a[2:].astype(BF)
    sum_b = sum_b[:, :2] + got_b.astype(F32)
    got_a = swap(send_a, z_neighbour)
    got_b = swap(sum_b[1].astype(BF), x_partner(1))
    kept = jnp.concatenate([sum_a[:2] + got_a.astype(F32), sum_b[0] + got_b.astype(F32)])

    index = lax.axis_index("pairs")
    group = index >> 3
    first, second = pair_order(lax.axis_index("sect"))

    def pick(value, at):
        return lax.dynamic_index_in_dim(value, at, 0, keepdims=False)

    send = jnp.stack([pick(kept, group ^ first), pick(kept, group ^ 2)]).astype(BF)
    got = swap(send, z_partner(0))
    got_last = swap((pick(kept, group ^ second) + got[1].astype(F32)).astype(BF), z_partner(1))
    own = pick(kept, group) + got[0].astype(F32) + got_last.astype(F32)
    used = lax.dynamic_index_in_dim(scalars, ROWS + (group >> 1), 0)
    row = (index & 15) * ROW + lax.broadcasted_iota(jnp.int32, (ROW, K), 0)
    return jnp.where(row < used[None, :], own, jnp.zeros((), F32)).astype(BF)


def solution(mesh):
    placed = (
        P("sect", None),
        P("pairs", "sect", None, None),
        P("pairs", "sect", None, None),
        P("pairs", None, None, None),
        P("pairs", None, None, None),
        P("pairs"),
        P("pairs"),
        P("sect"),
    )
    return jax.shard_map(
        local, mesh=mesh, in_specs=placed, out_specs=P(("sect", "pairs"), None), check_vma=False
    )
```

time: 362 us -> 62.9 us (0.17)
  waiting for transfers between devices: 237 us -> 28.7 us
  local copies, waits for them, and re-layouts: 62.2 us -> 0.68 us
  matrix products: 22.1 us -> 0 us
  other arithmetic: 19.6 us -> 1.91 us
  Pallas kernels: 0 us -> 15.1 us
  starting transfers between devices: 1.91 us -> 14.7 us
  between operations: 13.4 us -> 0.85 us
    reduce_scatter x1 -> x0, waiting for transfers between devices: 223 us -> none  [local(): lax.psum_scatter(normal_sum, 'pairs', scatter_dimension=0, tiled=True)]
    transpose x4 -> x0, local copies, waits for them, and re-layouts: 29.2 us -> none  [right_apply(): jnp.einsum('sikb,kcb->sikc', rolled, right_ops, preferred_element_type=jn...]
    while x32 -> x0, local copies, waits for them, and re-layouts: 24.9 us -> none
    dot_general x8 -> x0, matrix products: 22.1 us -> none  [the longest x4 13.2 us: right_apply(): jnp.einsum('sikb,kcb->sikc', rolled, right_ops, preferred_element_type=jn...]
    pallas_call x0 -> x5, Pallas kernels: none -> 15.1 us  [the longest x1 7.07 us: upper_call(): pl.pallas_call(body, name='upper', out_shape=(jax.ShapeDtypeStruct((2, 4,...]
    ppermute x1 -> x9, waiting for transfers between devices: 14.5 us -> 28.7 us  [the longest x8 25.2 us: swap(): return lax.ppermute(value, ('pairs', 'sect'), moves)]
    ppermute x1 -> x9, starting transfers between devices: 1.91 us -> 14.7 us  [the longest x8 12.8 us: swap(): return lax.ppermute(value, ('pairs', 'sect'), moves)]
    add x5 -> x6, other arithmetic: 12.7 us -> 0.44 us  [the longest x1 0.15 us: local(): sum_b = keep_b + got_b.astype(F32)]
  transfers between devices with their start and end apart: 2 -> 9, of which waited for: 2 -> 8; matrix products, arithmetic and copies ran while one was open for 0% -> 2% of each run, Pallas kernels for 0% -> 22%
where the time goes in v2:
time: 62.9 us; the launch traced here: 61.9 us
  waiting for transfers between devices  28.7 us (46%)
  Pallas kernels  15.1 us (24%)
  starting transfers between devices  14.7 us (23%)
  other arithmetic  1.91 us (3%)
  between operations  0.85 us (1%)
  local copies, waits for them, and re-layouts  0.68 us (1%)
    ppermute x8, waiting for transfers between devices, swap(): return lax.ppermute(value, ('pairs', 'sect'), moves)  25.2 us
    ppermute x8, starting transfers between devices, swap(): return lax.ppermute(value, ('pairs', 'sect'), moves)  12.8 us
    pallas_call x1, Pallas kernels, upper_call(): pl.pallas_call(body, name='upper', out_shape=(jax.ShapeDtypeStruct((2, 4,...  7.07 us
    pallas_call x2, Pallas kernels, lower_comp(): pl.pallas_call(body, name=name, out_shape=jax.ShapeDtypeStruct((2, 4, ROW...  3.9 us
    ppermute x1, waiting for transfers between devices, local(): lower = lax.ppermute(last, 'sect', [(i, i + 1) for i in range(sects - 1)])  3.46 us
    pallas_call x1, Pallas kernels, lower_normal(): pl.pallas_call(body, name='lower_normal', out_shape=jax.ShapeDtypeStruct(...  2.91 us
    ppermute x1, starting transfers between devices, local(): lower = lax.ppermute(last, 'sect', [(i, i + 1) for i in range(sects - 1)])  1.92 us
  transfers between devices with their start and end apart: 9, of which 8 were waited for; matrix products, arithmetic and copies ran while one was open for 2% of the time, Pallas kernels for 22%

profile of v2, /device:TPU:56, one launch (start us, length us, event | category | flops | bytes accessed | tf_op | source)
XLA Modules:
  0.0 61.9 jit_solution(1683957998268195070)
XLA Ops:
  0.0 1.3 %mask_last.1.m_b = bf16[512,1024]{1,0:T(8,128)(2,1)S(1)} custom-call(s32[2]{0:T(128)} %rows_ref.3, bf16[1024,1024]{1,0:T(8,128)(2,1)} %wave.3), custom_call_target="tpu_custom_call" | custom-call | flops 524288 | bytes 2097152 | tf_op jit(solution)/shard_map/mask_last/pallas_call | solution.py:89
  1.3 1.9 %collective-permute-start = (bf16[512,1024]{1,0:T(8,128)(2,1)S(1)}, bf16[512,1024]{1,0:T(8,128)(2,1)S(1)}, u32[]{:S(2)}, u32[]{:S(2)}) collective-permute-start(bf16[512,1024]{1,0:T(8,128)(2,1)S(1)} %mask_last.1.m_b), channel_id=1, source_target_pairs={{0,1},{1,2},{2,3},{3,4},{4,5},{5,6},{6,7},{8,9},{9,10},{10,11},{11... | collective-permute-start | bytes 3145736 | tf_op jit(solution)/shard_map/ppermute | solution.py:342
  3.8 7.1 %upper.1 = (f32[2,4,32,1024]{3,2,1,0:T(8,128)S(1)}, bf16[2,4,32,1024]{3,2,1,0:T(8,128)(2,1)S(1)}, s32[8]{0:T(128)S(1)}, bf16[512,1024]{1,0:T(8,128)(2,1)S(1)}, b...) custom-call(s32[1]{0:T(128)S(6)} %copy.9.cnt, s32[2]{0:T(128)} %shift_ref.1, ...), custom_call_target="tpu_custom_call" | custom-call | flops 4294967296 | bytes 10485760 | tf_op jit(solution)/shard_map/upper/pallas_call | solution.py:186
  11.0 2.9 %lower_normal.1.part = f32[2,16,32,512]{3,2,1,0:T(8,128)S(1)} custom-call(s32[8]{0:T(128)S(1)} %get-tuple-element.16.scal, bf16[512,1024]{1,0:T(8,128)(2,1)S(1)} %get-tuple-element.19.src, bf16[1024,512]{1,0:T(8,128)(2,1)S(1)} %get-tuple-element.20.lft, bf16[2,512,2048]{2,1,0:T(8,128)(2,1)S(1)} %get-tuple-element.18.rgt), custom_call_target="tpu_custom_call" | custom-call | flops 2147483648 | bytes 4194304 | tf_op jit(solution)/shard_map/lower_normal/pallas_call | solution.py:244
  13.9 3.5 %collective-permute-done.src = bf16[512,1024]{1,0:T(8,128)(2,1)S(1)} collective-permute-done((bf16[512,1024]{1,0:T(8,128)(2,1)S(1)}, bf16[512,1024]{1,0:T(8,128)(2,1)S(1)}, u32[]{:S(2)}, u32[]{:S(2)}) %collective-permute-start) | collective-permute-done | bytes 1048608 | tf_op jit(solution)/shard_map/ppermute | solution.py:342
  17.4 1.9 %lower_send.1 = bf16[2,4,32,1024]{3,2,1,0:T(8,128)(2,1)S(1)} custom-call(s32[8]{0:T(128)S(1)} %get-tuple-element.16.scal, bf16[512,1024]{1,0:T(8,128)(2,1)S(1)} %collective-permute-done.src, bf16[32,32,512]{2,1,0:T(8,128)(2,1)S(1)} %get-tuple-element.17.lft, bf16[2,512,2048]{2,1,0:T(8,128)(2,1)S(1)} %get-tuple-element.18.rgt, ...), custom_call_target="tpu_custom_call" | custom-call | flops 1073741824 | bytes 4194304 | tf_op jit(solution)/shard_map/lower_send/pallas_call | solution.py:271
  19.2 1.1 %collective-permute-start.1 = (bf16[2,4,32,1024]{3,2,1,0:T(8,128)(2,1)S(1)}, bf16[2,4,32,1024]{3,2,1,0:T(8,128)(2,1)S(1)}, u32[]{:S(2)}, u32[]{:S(2)}) collective-permute-start(bf16[2,4,32,1024]{3,2,1,0:T(8,128)(2,1)S(1)} %lower_send.1), channel_id=1, source_target_pairs={{0,8},{1,25},{2,10},{3,27},{4,12},{5,29},{6,14},{7,31},{8,0},{9,17... | collective-permute-start | bytes 1572872 | tf_op jit(solution)/shard_map/ppermute | solution.py:307
  20.3 2.0 %lower_keep.1 = f32[2,4,32,1024]{3,2,1,0:T(8,128)S(1)} custom-call(s32[8]{0:T(128)S(1)} %get-tuple-element.16.scal, bf16[512,1024]{1,0:T(8,128)(2,1)S(1)} %collective-permute-done.src, bf16[32,32,512]{2,1,0:T(8,128)(2,1)S(1)} %get-tuple-element.17.lft, bf16[2,512,2048]{2,1,0:T(8,128)(2,1)S(1)} %get-tuple-element.18.rgt, f32[2,16,32,512]{3,2,1,0:T(8,128)S(1)} %lower_normal.1.part), custom_call_target="tpu_custom_call" | custom-call | flops 1073741824 | bytes 4194304 | tf_op jit(solution)/shard_map/lower_keep/pallas_call | solution.py:271
  22.4 6.6 %collective-permute-done.1 = bf16[2,4,32,1024]{3,2,1,0:T(8,128)(2,1)S(1)} collective-permute-done((bf16[2,4,32,1024]{3,2,1,0:T(8,128)(2,1)S(1)}, bf16[2,4,32,1024]{3,2,1,0:T(8,128)(2,1)S(1)}, u32[]{:S(2)}, u32[]{:S(2)}) %collective-permute-start.1) | collective-permute-done | bytes 524320 | tf_op jit(solution)/shard_map/ppermute | solution.py:307
  29.0 0.1 convert_add_fusion.1
  29.2 3.7 %collective-permute-start.3 = (bf16[4,32,1024]{2,1,0:T(8,128)(2,1)S(1)}, bf16[4,32,1024]{2,1,0:T(8,128)(2,1)S(1)}, u32[]{:S(2)}, u32[]{:S(2)}) collective-permute-start(bf16[4,32,1024]{2,1,0:T(8,128)(2,1)S(1)} %fusion.1), channel_id=1, source_target_pairs={{0,24},{1,9},{2,26},{3,11},{4,28},{5,13},{6,30},{7,15},{8,16},{9,1... | collective-permute-start | bytes 786440 | tf_op jit(solution)/shard_map/ppermute | solution.py:307
  32.9 0.1 convert_add_fusion
  33.2 4.0 %collective-permute-done.3 = bf16[4,32,1024]{2,1,0:T(8,128)(2,1)S(1)} collective-permute-done((bf16[4,32,1024]{2,1,0:T(8,128)(2,1)S(1)}, bf16[4,32,1024]{2,1,0:T(8,128)(2,1)S(1)}, u32[]{:S(2)}, u32[]{:S(2)}) %collective-permute-start.3) | collective-permute-done | bytes 262176 | tf_op jit(solution)/shard_map/ppermute | solution.py:307
  37.2 2.3 %collective-permute-done.4 = bf16[2,2,32,1024]{3,2,1,0:T(8,128)(2,1)S(1)} collective-permute-done((bf16[2,2,32,1024]{3,2,1,0:T(8,128)(2,1)S(1)}, bf16[2,2,32,1024]{3,2,1,0:T(8,128)(2,1)S(1)}, u32[]{:S(2)}, u32[]{:S(2)}) %collective-permute-start.4) | collective-permute-done | bytes 262176 | tf_op jit(solution)/shard_map/ppermute | solution.py:307
  39.6 1.0 %collective-permute-start.6 = (bf16[2,32,1024]{2,1,0:T(8,128)(2,1)S(1)}, bf16[2,32,1024]{2,1,0:T(8,128)(2,1)S(1)}, u32[]{:S(2)}, u32[]{:S(2)}) collective-permute-start(bf16[2,32,1024]{2,1,0:T(8,128)(2,1)S(1)} %fusion.3), channel_id=1, source_target_pairs={{0,24},{1,9},{2,26},{3,11},{4,28},{5,13},{6,30},{7,15},{8,16},{9,1... | collective-permute-start | bytes 393224 | tf_op jit(solution)/shard_map/ppermute | solution.py:307
  40.8 5.1 %collective-permute-done.6 = bf16[2,32,1024]{2,1,0:T(8,128)(2,1)S(1)} collective-permute-done((bf16[2,32,1024]{2,1,0:T(8,128)(2,1)S(1)}, bf16[2,32,1024]{2,1,0:T(8,128)(2,1)S(1)}, u32[]{:S(2)}, u32[]{:S(2)}) %collective-permute-start.6) | collective-permute-done | bytes 131104 | tf_op jit(solution)/shard_map/ppermute | solution.py:307
  45.9 0.9 %collective-permute-done.5 = bf16[2,32,1024]{2,1,0:T(8,128)(2,1)S(1)} collective-permute-done((bf16[2,32,1024]{2,1,0:T(8,128)(2,1)S(1)}, bf16[2,32,1024]{2,1,0:T(8,128)(2,1)S(1)}, u32[]{:S(2)}, u32[]{:S(2)}) %collective-permute-start.5) | collective-permute-done | bytes 131104 | tf_op jit(solution)/shard_map/ppermute | solution.py:307
  46.9 1.7 %collective-permute-start.7 = (bf16[2,32,1024]{2,1,0:T(8,128)(2,1)S(1)}, bf16[2,32,1024]{2,1,0:T(8,128)(2,1)S(1)}, u32[]{:S(2)}, u32[]{:S(2)}) collective-permute-start(bf16[2,32,1024]{2,1,0:T(8,128)(2,1)S(1)} %pad_maximum_fusion), channel_id=1, source_target_pairs={{0,64},{1,193},{2,66},{3,195},{4,68},{5,197},{6,70},{7,199},{8,72}... | collective-permute-start | bytes 393224 | tf_op jit(solution)/shard_map/ppermute | solution.py:307
  48.6 0.6 dynamic_slice.17
  49.2 4.7 %collective-permute-done.7 = bf16[2,32,1024]{2,1,0:T(8,128)(2,1)S(1)} collective-permute-done((bf16[2,32,1024]{2,1,0:T(8,128)(2,1)S(1)}, bf16[2,32,1024]{2,1,0:T(8,128)(2,1)S(1)}, u32[]{:S(2)}, u32[]{:S(2)}) %collective-permute-start.7) | collective-permute-done | bytes 131104 | tf_op jit(solution)/shard_map/ppermute | solution.py:307
  53.9 5.0 %collective-permute-start.8 = (bf16[32,1024]{1,0:T(8,128)(2,1)S(1)}, bf16[32,1024]{1,0:T(8,128)(2,1)S(1)}, u32[]{:S(2)}, u32[]{:S(2)}) collective-permute-start(bf16[32,1024]{1,0:T(8,128)(2,1)S(1)} %fusion.17), channel_id=1, source_target_pairs={{0,192},{1,65},{2,194},{3,67},{4,196},{5,69},{6,198},{7,71},{8,200... | collective-permute-start | bytes 196616 | tf_op jit(solution)/shard_map/ppermute | solution.py:307
  58.9 0.7 %add_compare_fusion = pred[32]{0:T(512)(128)(4,1)S(1)} fusion(s32[]{:T(128)} %bitcast.1, s32[]{:T(128)S(6)} %mul.7), kind=kLoop, calls=%fused_computation.37 | loop fusion | flops 64 | bytes 40 | tf_op jit(solution)/shard_map/lt | solution.py:388
  59.6 1.6 %collective-permute-done.8 = bf16[32,1024]{1,0:T(8,128)(2,1)S(1)} collective-permute-done((bf16[32,1024]{1,0:T(8,128)(2,1)S(1)}, bf16[32,1024]{1,0:T(8,128)(2,1)S(1)}, u32[]{:S(2)}, u32[]{:S(2)}) %collective-permute-start.8) | collective-permute-done | bytes 65568 | tf_op jit(solution)/shard_map/ppermute | solution.py:307
  61.2 0.7 %fusion.12 = bf16[32,1024]{1,0:T(8,128)(2,1)} fusion(s32[]{:T(128)S(6)} %select_n.22, f32[2,32,1024]{2,1,0:T(8,128)S(1)} %slice_add_fusion.1, f32[2,32,1024]{2,1,0:T(8,128)S(1)} %fusion.2, bf16[32,1024]{1,0:T(8,128)(2,1)S(1)} %collective-permute-done.8, bf16[2,32,1024]{2,1,0:T(8,128)(2,1)S(1)} %collective-permute-done.7, pred[32]{0:T(512)(128)(4,1)S(1)} %add_compare_fusion), kind=kLoop, calls=%fused_computation.30 | loop fusion | flops 229376 | bytes 720932 | tf_op jit(solution)/shard_map/convert_element_type | solution.py:388
  (15 shorter events, 0.6 us)
Async XLA Ops:
  1.3 16.1 %collective-permute-start = (bf16[512,1024]{1,0:T(8,128)(2,1)S(1)}, bf16[512,1024]{1,0:T(8,128)(2,1)S(1)}, u32[]{:S(2)}, u32[]{:S(2)}) collective-permute-start(bf16[512,1024]{1,0:T(8,128)(2,1)S(1)} %mask_last.1.m_b), channel_id=1, source_target_pairs={{0,1},{1,2},{2,3},{3,4},{4,5},{5,6},{6,7},{8,9},{9,10},{10,11},{11... | collective-permute-start | bytes 3145736 | tf_op jit(solution)/shard_map/ppermute | solution.py:342
  10.9 11.5 %collective-permute-start.2 = (bf16[2,4,32,1024]{3,2,1,0:T(8,128)(2,1)S(1)}, bf16[2,4,32,1024]{3,2,1,0:T(8,128)(2,1)S(1)}, u32[]{:S(2)}, u32[]{:S(2)}) collective-permute-start(bf16[2,4,32,1024]{3,2,1,0:T(8,128)(2,1)S(1)} %get-tuple-element.21), channel_id=1, source_target_pairs={{0,8},{1,25},{2,10},{3,27},{4,12},{5,29},{6,14},{7,31},{8,0},{9,17... | collective-permute-start | bytes 1572872 | tf_op jit(solution)/shard_map/ppermute | solution.py:307
  19.2 9.8 %collective-permute-start.1 = (bf16[2,4,32,1024]{3,2,1,0:T(8,128)(2,1)S(1)}, bf16[2,4,32,1024]{3,2,1,0:T(8,128)(2,1)S(1)}, u32[]{:S(2)}, u32[]{:S(2)}) collective-permute-start(bf16[2,4,32,1024]{3,2,1,0:T(8,128)(2,1)S(1)} %lower_send.1), channel_id=1, source_target_pairs={{0,8},{1,25},{2,10},{3,27},{4,12},{5,29},{6,14},{7,31},{8,0},{9,17... | collective-permute-start | bytes 1572872 | tf_op jit(solution)/shard_map/ppermute | solution.py:307
  29.2 8.0 %collective-permute-start.3 = (bf16[4,32,1024]{2,1,0:T(8,128)(2,1)S(1)}, bf16[4,32,1024]{2,1,0:T(8,128)(2,1)S(1)}, u32[]{:S(2)}, u32[]{:S(2)}) collective-permute-start(bf16[4,32,1024]{2,1,0:T(8,128)(2,1)S(1)} %fusion.1), channel_id=1, source_target_pairs={{0,24},{1,9},{2,26},{3,11},{4,28},{5,13},{6,30},{7,15},{8,16},{9,1... | collective-permute-start | bytes 786440 | tf_op jit(solution)/shard_map/ppermute | solution.py:307
  33.1 6.5 %collective-permute-start.4 = (bf16[2,2,32,1024]{3,2,1,0:T(8,128)(2,1)S(1)}, bf16[2,2,32,1024]{3,2,1,0:T(8,128)(2,1)S(1)}, u32[]{:S(2)}, u32[]{:S(2)}) collective-permute-start(bf16[2,2,32,1024]{3,2,1,0:T(8,128)(2,1)S(1)} %slice.74), channel_id=1, source_target_pairs={{0,32},{1,225},{2,34},{3,227},{4,36},{5,229},{6,38},{7,231},{8,40}... | collective-permute-start | bytes 786440 | tf_op jit(solution)/shard_map/ppermute | solution.py:307
  39.6 6.3 %collective-permute-start.6 = (bf16[2,32,1024]{2,1,0:T(8,128)(2,1)S(1)}, bf16[2,32,1024]{2,1,0:T(8,128)(2,1)S(1)}, u32[]{:S(2)}, u32[]{:S(2)}) collective-permute-start(bf16[2,32,1024]{2,1,0:T(8,128)(2,1)S(1)} %fusion.3), channel_id=1, source_target_pairs={{0,24},{1,9},{2,26},{3,11},{4,28},{5,13},{6,30},{7,15},{8,16},{9,1... | collective-permute-start | bytes 393224 | tf_op jit(solution)/shard_map/ppermute | solution.py:307
  40.7 6.1 %collective-permute-start.5 = (bf16[2,32,1024]{2,1,0:T(8,128)(2,1)S(1)}, bf16[2,32,1024]{2,1,0:T(8,128)(2,1)S(1)}, u32[]{:S(2)}, u32[]{:S(2)}) collective-permute-start(bf16[2,32,1024]{2,1,0:T(8,128)(2,1)S(1)} %slice.75), channel_id=1, source_target_pairs={{0,32},{1,225},{2,34},{3,227},{4,36},{5,229},{6,38},{7,231},{8,40}... | collective-permute-start | bytes 393224 | tf_op jit(solution)/shard_map/ppermute | solution.py:307
  46.9 7.0 %collective-permute-start.7 = (bf16[2,32,1024]{2,1,0:T(8,128)(2,1)S(1)}, bf16[2,32,1024]{2,1,0:T(8,128)(2,1)S(1)}, u32[]{:S(2)}, u32[]{:S(2)}) collective-permute-start(bf16[2,32,1024]{2,1,0:T(8,128)(2,1)S(1)} %pad_maximum_fusion), channel_id=1, source_target_pairs={{0,64},{1,193},{2,66},{3,195},{4,68},{5,197},{6,70},{7,199},{8,72}... | collective-permute-start | bytes 393224 | tf_op jit(solution)/shard_map/ppermute | solution.py:307
  53.9 7.3 %collective-permute-start.8 = (bf16[32,1024]{1,0:T(8,128)(2,1)S(1)}, bf16[32,1024]{1,0:T(8,128)(2,1)S(1)}, u32[]{:S(2)}, u32[]{:S(2)}) collective-permute-start(bf16[32,1024]{1,0:T(8,128)(2,1)S(1)} %fusion.17), channel_id=1, source_target_pairs={{0,192},{1,65},{2,194},{3,67},{4,196},{5,69},{6,198},{7,71},{8,200... | collective-permute-start | bytes 196616 | tf_op jit(solution)/shard_map/ppermute | solution.py:307

commit v3 on v2

--- a/solution.py
+++ b/solution.py
@@ -207,7 +207,7 @@
             pltpu.SMEM((2,), jnp.int32),
             pltpu.SemaphoreType.DMA((15,)),
         ],
-        compiler_params=limit(28),
+        compiler_params=limit(20),
         cost_estimate=cost(2 * NP * 4 * B * B * K, 10),
     )(
         pair_count,
@@ -293,8 +293,8 @@
     return (x, z ^ 1) if sect & 1 == 0 else (x, (z + 1 if z & 1 else z - 1) % 8)
 
 
-def z_partner(step):
-    return lambda x, z, sect: (x, z ^ (2 * pair_order(sect)[step]))
+def z_group(mask):
+    return lambda x, z, sect: (x, z ^ (2 * mask))
 
 
 def swap(value, partner):
@@ -358,31 +358,29 @@
 
     got_b = swap(send_b, x_partner(0))
     got_a = swap(send_a, x_partner(0))
-    got_a, got_b = lax.optimization_barrier((got_a, got_b))
+    got_b, keep_a = lax.optimization_barrier((got_b, keep_a))
+    sum_b = keep_b + got_b.astype(F32)
+    got_b = swap(sum_b[:, 2:].astype(BF), z_neighbour)
     sum_a = keep_a + got_a.astype(F32)
     send_a = sum_a[1].astype(BF)
-    sum_b = keep_b + got_b.astype(F32)
-    got_a = swap(send_a, x_partner(1))
-    got_b = swap(sum_b[:, 2:].astype(BF), z_neighbour)
-    got_a, got_b = lax.optimization_barrier((got_a, got_b))
+    send_a, got_b = lax.optimization_barrier((send_a, got_b))
+    sum_b = sum_b[:, :2] + got_b.astype(F32)
+    got = swap(jnp.concatenate([send_a, sum_b[1].astype(BF)]), x_partner(1))
+    got_a, got_b = got[:4], got[4:]
     sum_a = sum_a[0] + got_a.astype(F32)
-    send_a = sum_a[2:].astype(BF)
-    sum_b = sum_b[:, :2] + got_b.astype(F32)
-    got_a = swap(send_a, z_neighbour)
-    got_b = swap(sum_b[1].astype(BF), x_partner(1))
+    got_a = swap(sum_a[2:].astype(BF), z_neighbour)
     kept = jnp.concatenate([sum_a[:2] + got_a.astype(F32), sum_b[0] + got_b.astype(F32)])
 
     index = lax.axis_index("pairs")
     group = index >> 3
-    first, second = pair_order(lax.axis_index("sect"))
 
     def pick(value, at):
         return lax.dynamic_index_in_dim(value, at, 0, keepdims=False)
 
-    send = jnp.stack([pick(kept, group ^ first), pick(kept, group ^ 2)]).astype(BF)
-    got = swap(send, z_partner(0))
-    got_last = swap((pick(kept, group ^ second) + got[1].astype(F32)).astype(BF), z_partner(1))
-    own = pick(kept, group) + got[0].astype(F32) + got_last.astype(F32)
+    own = pick(kept, group)
+    for mask in (2, 3, 1):
+        got = swap(pick(kept, group ^ mask).astype(BF), z_group(mask))
+        own = own + got.astype(F32)
     used = lax.dynamic_index_in_dim(scalars, ROWS + (group >> 1), 0)
     row = (index & 15) * ROW + lax.broadcasted_iota(jnp.int32, (ROW, K), 0)
     return jnp.where(row < used[None, :], own, jnp.zeros((), F32)).astype(BF)

time: 62.9 us -> 59.6 us (0.948); the launches traced: 61.9 us -> 59.3 us
  waiting for transfers between devices: 28.7 us -> 25.3 us
  starting transfers between devices: 14.7 us -> 15.5 us
    ppermute x8, waiting for transfers between devices: 25.2 us -> 21.8 us  [swap(): return lax.ppermute(value, ('pairs', 'sect'), moves)]
    ppermute x8, starting transfers between devices: 12.8 us -> 13.6 us  [swap(): return lax.ppermute(value, ('pairs', 'sect'), moves)]
  transfers between devices with their start and end apart: 9 -> 9, of which waited for: 8 -> 7; matrix products, arithmetic and copies ran while one was open for 2% -> 3% of each run, Pallas kernels for 22% -> 23%
where the time goes in v3:
time: 59.6 us; the launch traced here: 59.3 us
  waiting for transfers between devices  25.3 us (42%)
  starting transfers between devices  15.5 us (26%)
  Pallas kernels  15.1 us (25%)
  other arithmetic  1.96 us (3%)
  between operations  0.81 us (1%)
  local copies, waits for them, and re-layouts  0.68 us (1%)
    ppermute x8, waiting for transfers between devices, swap(): return lax.ppermute(value, ('pairs', 'sect'), moves)  21.8 us
    ppermute x8, starting transfers between devices, swap(): return lax.ppermute(value, ('pairs', 'sect'), moves)  13.6 us
    pallas_call x1, Pallas kernels, upper_call(): pl.pallas_call(body, name='upper', out_shape=(jax.ShapeDtypeStruct((2, 4,...  7.05 us
    pallas_call x2, Pallas kernels, lower_comp(): pl.pallas_call(body, name=name, out_shape=jax.ShapeDtypeStruct((2, 4, ROW...  3.89 us
    ppermute x1, waiting for transfers between devices, local(): lower = lax.ppermute(last, 'sect', [(i, i + 1) for i in range(sects - 1)])  3.47 us
    pallas_call x1, Pallas kernels, lower_normal(): pl.pallas_call(body, name='lower_normal', out_shape=jax.ShapeDtypeStruct(...  2.91 us
    ppermute x1, starting transfers between devices, local(): lower = lax.ppermute(last, 'sect', [(i, i + 1) for i in range(sects - 1)])  1.92 us
    pallas_call x1, Pallas kernels, mask_last(): pl.pallas_call(body, name='mask_last', out_shape=jax.ShapeDtypeStruct((B,...  1.25 us
  transfers between devices with their start and end apart: 9, of which 7 were waited for; matrix products, arithmetic and copies ran while one was open for 3% of the time, Pallas kernels for 23%

profile of v3, /device:TPU:56, one launch (start us, length us, event | category | flops | bytes accessed | tf_op | source)
XLA Modules:
  0.0 59.3 jit_solution(1595744730863340211)
XLA Ops:
  0.0 1.3 %mask_last.1.m_b = bf16[512,1024]{1,0:T(8,128)(2,1)S(1)} custom-call(s32[2]{0:T(128)} %rows_ref.3, bf16[1024,1024]{1,0:T(8,128)(2,1)} %wave.3), custom_call_target="tpu_custom_call" | custom-call | flops 524288 | bytes 2097152 | tf_op jit(solution)/shard_map/mask_last/pallas_call | solution.py:89
  1.3 1.9 %collective-permute-start.1 = (bf16[512,1024]{1,0:T(8,128)(2,1)S(1)}, bf16[512,1024]{1,0:T(8,128)(2,1)S(1)}, u32[]{:S(2)}, u32[]{:S(2)}) collective-permute-start(bf16[512,1024]{1,0:T(8,128)(2,1)S(1)} %mask_last.1.m_b), channel_id=1, source_target_pairs={{0,1},{1,2},{2,3},{3,4},{4,5},{5,6},{6,7},{8,9},{9,10},{10,11},{11... | collective-permute-start | bytes 3145736 | tf_op jit(solution)/shard_map/ppermute | solution.py:342
  3.8 7.0 %upper.1 = (f32[2,4,32,1024]{3,2,1,0:T(8,128)S(1)}, bf16[2,4,32,1024]{3,2,1,0:T(8,128)(2,1)S(1)}, s32[8]{0:T(128)S(1)}, bf16[512,1024]{1,0:T(8,128)(2,1)S(1)}, b...) custom-call(s32[1]{0:T(128)S(6)} %copy.9.cnt, s32[2]{0:T(128)} %shift_ref.1, ...), custom_call_target="tpu_custom_call" | custom-call | flops 4294967296 | bytes 10485760 | tf_op jit(solution)/shard_map/upper/pallas_call | solution.py:186
  11.0 2.9 %lower_normal.1.part = f32[2,16,32,512]{3,2,1,0:T(8,128)S(1)} custom-call(s32[8]{0:T(128)S(1)} %get-tuple-element.16.scal, bf16[512,1024]{1,0:T(8,128)(2,1)S(1)} %get-tuple-element.20.src, bf16[1024,512]{1,0:T(8,128)(2,1)S(1)} %get-tuple-element.21.lft, bf16[2,512,2048]{2,1,0:T(8,128)(2,1)S(1)} %get-tuple-element.19.rgt), custom_call_target="tpu_custom_call" | custom-call | flops 2147483648 | bytes 4194304 | tf_op jit(solution)/shard_map/lower_normal/pallas_call | solution.py:244
  13.9 3.5 %collective-permute-done.1.src = bf16[512,1024]{1,0:T(8,128)(2,1)S(1)} collective-permute-done((bf16[512,1024]{1,0:T(8,128)(2,1)S(1)}, bf16[512,1024]{1,0:T(8,128)(2,1)S(1)}, u32[]{:S(2)}, u32[]{:S(2)}) %collective-permute-start.1) | collective-permute-done | bytes 1048608 | tf_op jit(solution)/shard_map/ppermute | solution.py:342
  17.4 1.9 %lower_send.1 = bf16[2,4,32,1024]{3,2,1,0:T(8,128)(2,1)S(1)} custom-call(s32[8]{0:T(128)S(1)} %get-tuple-element.16.scal, bf16[512,1024]{1,0:T(8,128)(2,1)S(1)} %collective-permute-done.1.src, bf16[32,32,512]{2,1,0:T(8,128)(2,1)S(1)} %get-tuple-element.18.lft, bf16[2,512,2048]{2,1,0:T(8,128)(2,1)S(1)} %get-tuple-element.19.rgt, ...), custom_call_target="tpu_custom_call" | custom-call | flops 1073741824 | bytes 4194304 | tf_op jit(solution)/shard_map/lower_send/pallas_call | solution.py:271
  19.2 1.1 %collective-permute-start.2 = (bf16[2,4,32,1024]{3,2,1,0:T(8,128)(2,1)S(1)}, bf16[2,4,32,1024]{3,2,1,0:T(8,128)(2,1)S(1)}, u32[]{:S(2)}, u32[]{:S(2)}) collective-permute-start(bf16[2,4,32,1024]{3,2,1,0:T(8,128)(2,1)S(1)} %lower_send.1), channel_id=1, source_target_pairs={{0,8},{1,25},{2,10},{3,27},{4,12},{5,29},{6,14},{7,31},{8,0},{9,17... | collective-permute-start | bytes 1572872 | tf_op jit(solution)/shard_map/ppermute | solution.py:307
  20.3 2.0 %lower_keep.1 = f32[2,4,32,1024]{3,2,1,0:T(8,128)S(1)} custom-call(s32[8]{0:T(128)S(1)} %get-tuple-element.16.scal, bf16[512,1024]{1,0:T(8,128)(2,1)S(1)} %collective-permute-done.1.src, bf16[32,32,512]{2,1,0:T(8,128)(2,1)S(1)} %get-tuple-element.18.lft, bf16[2,512,2048]{2,1,0:T(8,128)(2,1)S(1)} %get-tuple-element.19.rgt, ...), custom_call_target="tpu_custom_call" | custom-call | flops 1073741824 | bytes 4194304 | tf_op jit(solution)/shard_map/lower_keep/pallas_call | solution.py:271
  22.4 0.2 convert_add_fusion
  22.6 0.2 collective-permute-start.3
  22.8 5.7 %collective-permute-done.2 = bf16[2,4,32,1024]{3,2,1,0:T(8,128)(2,1)S(1)} collective-permute-done((bf16[2,4,32,1024]{3,2,1,0:T(8,128)(2,1)S(1)}, bf16[2,4,32,1024]{3,2,1,0:T(8,128)(2,1)S(1)}, u32[]{:S(2)}, u32[]{:S(2)}) %collective-permute-start.2) | collective-permute-done | bytes 524320 | tf_op jit(solution)/shard_map/ppermute | solution.py:307
  28.5 0.1 convert_add_fusion.1
  28.7 0.4 collective-permute-done.3
  29.2 2.7 %collective-permute-start.4 = (bf16[6,32,1024]{2,1,0:T(8,128)(2,1)S(1)}, bf16[6,32,1024]{2,1,0:T(8,128)(2,1)S(1)}, u32[]{:S(2)}, u32[]{:S(2)}) collective-permute-start(bf16[6,32,1024]{2,1,0:T(8,128)(2,1)S(1)} %pad_maximum_fusion), channel_id=1, source_target_pairs={{0,24},{1,9},{2,26},{3,11},{4,28},{5,13},{6,30},{7,15},{8,16},{9,1... | collective-permute-start | bytes 1179656 | tf_op jit(solution)/shard_map/ppermute | solution.py:307
  31.9 0.6 dynamic_slice.17
  32.5 5.8 %collective-permute-done.4 = bf16[6,32,1024]{2,1,0:T(8,128)(2,1)S(1)} collective-permute-done((bf16[6,32,1024]{2,1,0:T(8,128)(2,1)S(1)}, bf16[6,32,1024]{2,1,0:T(8,128)(2,1)S(1)}, u32[]{:S(2)}, u32[]{:S(2)}) %collective-permute-start.4) | collective-permute-done | bytes 393248 | tf_op jit(solution)/shard_map/ppermute | solution.py:307
  38.4 0.2 collective-permute-start.5
  38.6 4.8 %collective-permute-done.5 = bf16[2,32,1024]{2,1,0:T(8,128)(2,1)S(1)} collective-permute-done((bf16[2,32,1024]{2,1,0:T(8,128)(2,1)S(1)}, bf16[2,32,1024]{2,1,0:T(8,128)(2,1)S(1)}, u32[]{:S(2)}, u32[]{:S(2)}) %collective-permute-start.5) | collective-permute-done | bytes 131104 | tf_op jit(solution)/shard_map/ppermute | solution.py:307
  43.6 8.7 %collective-permute-start.6 = (bf16[32,1024]{1,0:T(8,128)(2,1)S(1)}, bf16[32,1024]{1,0:T(8,128)(2,1)S(1)}, u32[]{:S(2)}, u32[]{:S(2)}) collective-permute-start(bf16[32,1024]{1,0:T(8,128)(2,1)S(1)} %get-tuple-element.27), channel_id=1, source_target_pairs={{0,128},{1,129},{2,130},{3,131},{4,132},{5,133},{6,134},{7,135},{8... | collective-permute-start | bytes 196616 | tf_op jit(solution)/shard_map/ppermute | solution.py:307
  52.2 0.7 %collective-permute-start.8 = (bf16[32,1024]{1,0:T(8,128)(2,1)S(1)}, bf16[32,1024]{1,0:T(8,128)(2,1)S(1)}, u32[]{:S(2)}, u32[]{:S(2)}) collective-permute-start(bf16[32,1024]{1,0:T(8,128)(2,1)S(1)} %get-tuple-element.29), channel_id=1, source_target_pairs={{0,64},{1,65},{2,66},{3,67},{4,68},{5,69},{6,70},{7,71},{8,72},{9,... | collective-permute-start | bytes 196616 | tf_op jit(solution)/shard_map/ppermute | solution.py:307
  52.9 0.7 %add_compare_fusion = pred[32]{0:T(512)(128)(4,1)S(1)} fusion(s32[]{:T(128)} %bitcast.1, s32[]{:T(128)S(6)} %mul.3), kind=kLoop, calls=%fused_computation.39 | loop fusion | flops 64 | bytes 40 | tf_op jit(solution)/shard_map/lt | solution.py:386
  53.5 1.8 %collective-permute-done.6 = bf16[32,1024]{1,0:T(8,128)(2,1)S(1)} collective-permute-done((bf16[32,1024]{1,0:T(8,128)(2,1)S(1)}, bf16[32,1024]{1,0:T(8,128)(2,1)S(1)}, u32[]{:S(2)}, u32[]{:S(2)}) %collective-permute-start.6) | collective-permute-done | bytes 65568 | tf_op jit(solution)/shard_map/ppermute | solution.py:307
  55.4 3.2 %collective-permute-done.7 = bf16[32,1024]{1,0:T(8,128)(2,1)S(1)} collective-permute-done((bf16[32,1024]{1,0:T(8,128)(2,1)S(1)}, bf16[32,1024]{1,0:T(8,128)(2,1)S(1)}, u32[]{:S(2)}, u32[]{:S(2)}) %collective-permute-start.7) | collective-permute-done | bytes 65568 | tf_op jit(solution)/shard_map/ppermute | solution.py:307
  58.6 0.7 %fusion.12 = bf16[32,1024]{1,0:T(8,128)(2,1)} fusion(s32[]{:T(128)S(6)} %select_n.22, f32[2,32,1024]{2,1,0:T(8,128)S(1)} %slice_add_fusion.1, f32[2,32,1024]{2,1,0:T(8,128)S(1)} %fusion.2, bf16[32,1024]{1,0:T(8,128)(2,1)S(1)} %collective-permute-done.8, bf16[32,1024]{1,0:T(8,128)(2,1)S(1)} %collective-permute-done.7, ...), kind=kLoop, calls=%fused_computation.31 | loop fusion | flops 294912 | bytes 786468 | tf_op jit(solution)/shard_map/convert_element_type | solution.py:386
  (14 shorter events, 0.5 us)
Async XLA Ops:
  1.3 16.1 %collective-permute-start.1 = (bf16[512,1024]{1,0:T(8,128)(2,1)S(1)}, bf16[512,1024]{1,0:T(8,128)(2,1)S(1)}, u32[]{:S(2)}, u32[]{:S(2)}) collective-permute-start(bf16[512,1024]{1,0:T(8,128)(2,1)S(1)} %mask_last.1.m_b), channel_id=1, source_target_pairs={{0,1},{1,2},{2,3},{3,4},{4,5},{5,6},{6,7},{8,9},{9,10},{10,11},{11... | collective-permute-start | bytes 3145736 | tf_op jit(solution)/shard_map/ppermute | solution.py:342
  10.9 11.5 %collective-permute-start = (bf16[2,4,32,1024]{3,2,1,0:T(8,128)(2,1)S(1)}, bf16[2,4,32,1024]{3,2,1,0:T(8,128)(2,1)S(1)}, u32[]{:S(2)}, u32[]{:S(2)}) collective-permute-start(bf16[2,4,32,1024]{3,2,1,0:T(8,128)(2,1)S(1)} %get-tuple-element.17), channel_id=1, source_target_pairs={{0,8},{1,25},{2,10},{3,27},{4,12},{5,29},{6,14},{7,31},{8,0},{9,17... | collective-permute-start | bytes 1572872 | tf_op jit(solution)/shard_map/ppermute | solution.py:307
  19.2 9.3 %collective-permute-start.2 = (bf16[2,4,32,1024]{3,2,1,0:T(8,128)(2,1)S(1)}, bf16[2,4,32,1024]{3,2,1,0:T(8,128)(2,1)S(1)}, u32[]{:S(2)}, u32[]{:S(2)}) collective-permute-start(bf16[2,4,32,1024]{3,2,1,0:T(8,128)(2,1)S(1)} %lower_send.1), channel_id=1, source_target_pairs={{0,8},{1,25},{2,10},{3,27},{4,12},{5,29},{6,14},{7,31},{8,0},{9,17... | collective-permute-start | bytes 1572872 | tf_op jit(solution)/shard_map/ppermute | solution.py:307
  22.6 6.5 %collective-permute-start.3 = (bf16[2,2,32,1024]{3,2,1,0:T(8,128)(2,1)S(1)}, bf16[2,2,32,1024]{3,2,1,0:T(8,128)(2,1)S(1)}, u32[]{:S(2)}, u32[]{:S(2)}) collective-permute-start(bf16[2,2,32,1024]{3,2,1,0:T(8,128)(2,1)S(1)} %slice.72), channel_id=1, source_target_pairs={{0,32},{1,225},{2,34},{3,227},{4,36},{5,229},{6,38},{7,231},{8,40}... | collective-permute-start | bytes 786440 | tf_op jit(solution)/shard_map/ppermute | solution.py:307
  29.2 9.1 %collective-permute-start.4 = (bf16[6,32,1024]{2,1,0:T(8,128)(2,1)S(1)}, bf16[6,32,1024]{2,1,0:T(8,128)(2,1)S(1)}, u32[]{:S(2)}, u32[]{:S(2)}) collective-permute-start(bf16[6,32,1024]{2,1,0:T(8,128)(2,1)S(1)} %pad_maximum_fusion), channel_id=1, source_target_pairs={{0,24},{1,9},{2,26},{3,11},{4,28},{5,13},{6,30},{7,15},{8,16},{9,1... | collective-permute-start | bytes 1179656 | tf_op jit(solution)/shard_map/ppermute | solution.py:307
  38.4 5.1 %collective-permute-start.5 = (bf16[2,32,1024]{2,1,0:T(8,128)(2,1)S(1)}, bf16[2,32,1024]{2,1,0:T(8,128)(2,1)S(1)}, u32[]{:S(2)}, u32[]{:S(2)}) collective-permute-start(bf16[2,32,1024]{2,1,0:T(8,128)(2,1)S(1)} %slice.73), channel_id=1, source_target_pairs={{0,32},{1,225},{2,34},{3,227},{4,36},{5,229},{6,38},{7,231},{8,40}... | collective-permute-start | bytes 393224 | tf_op jit(solution)/shard_map/ppermute | solution.py:307
  43.6 11.8 %collective-permute-start.6 = (bf16[32,1024]{1,0:T(8,128)(2,1)S(1)}, bf16[32,1024]{1,0:T(8,128)(2,1)S(1)}, u32[]{:S(2)}, u32[]{:S(2)}) collective-permute-start(bf16[32,1024]{1,0:T(8,128)(2,1)S(1)} %get-tuple-element.27), channel_id=1, source_target_pairs={{0,128},{1,129},{2,130},{3,131},{4,132},{5,133},{6,134},{7,135},{8... | collective-permute-start | bytes 196616 | tf_op jit(solution)/shard_map/ppermute | solution.py:307
  52.2 6.4 %collective-permute-start.7 = (bf16[32,1024]{1,0:T(8,128)(2,1)S(1)}, bf16[32,1024]{1,0:T(8,128)(2,1)S(1)}, u32[]{:S(2)}, u32[]{:S(2)}) collective-permute-start(bf16[32,1024]{1,0:T(8,128)(2,1)S(1)} %get-tuple-element.28), channel_id=1, source_target_pairs={{0,192},{1,193},{2,194},{3,195},{4,196},{5,197},{6,198},{7,199},{8... | collective-permute-start | bytes 196616 | tf_op jit(solution)/shard_map/ppermute | solution.py:307
  52.2 6.4 %collective-permute-start.8 = (bf16[32,1024]{1,0:T(8,128)(2,1)S(1)}, bf16[32,1024]{1,0:T(8,128)(2,1)S(1)}, u32[]{:S(2)}, u32[]{:S(2)}) collective-permute-start(bf16[32,1024]{1,0:T(8,128)(2,1)S(1)} %get-tuple-element.29), channel_id=1, source_target_pairs={{0,64},{1,65},{2,66},{3,67},{4,68},{5,69},{6,70},{7,71},{8,72},{9,... | collective-permute-start | bytes 196616 | tf_op jit(solution)/shard_map/ppermute | solution.py:307
